TPU v7x, 128 devices: a whole 4x4x4 slice. The times are simulated.
128 devices in a mesh: span: 8 (over x, y_lo), tok: 16 (over z, y_hi, core).
Axes of the slice: x: 4, y: 4 (y_hi: 2, y_lo: 2; y = y_hi * 2 + y_lo), z: 4, core: 2. Of those that a mesh axis runs over, the one named last changes fastest.
Arguments:
- latents: bfloat16 [8, 1024, 3584], P('span', 'tok'), may hold values from -6 to 6
- levels: int32 [8], P('span'), may hold values from 0 to 14
- visible: int32 [8, 8], replicated, may hold values 0 or 1
- frame_counts: int32 [8], replicated, may hold values from 0 to 2
- modulation: float32 [16, 3, 3584], replicated, may hold values from -4 to 4
- w_qkv: bfloat16 [3584, 3, 4096], P(None, None, 'tok')
- qk_gain: float32 [2, 4096], P(None, 'tok'), may hold values from 0 to 5
- w_out: bfloat16 [4096, 3584], P('tok'), may hold values from -0.09375 to 0.09375
- w_head: bfloat16 [3584, 96], replicated, may hold values from -0.09375 to 0.09375
- conv_w: bfloat16 [3, 96, 384], replicated, may hold values from -0.375 to 0.375
Outputs:
- denoised: bfloat16 [8, 1024, 3584], P('span', 'tok')
- decoded: bfloat16 [8, 1024, 384], P('span', 'tok')
All inputs are finite; a program needn't handle non-finite values.
Results may differ from a plain program's by a relative error of at most 0.015.
Values may be sent and summed in bfloat16 or wider, within the bound.
A program may use at most 128 MiB of HBM per device.

v0:
```python
import jax
import jax.numpy as jnp
from jax import lax
from jax.sharding import PartitionSpec as P

HD = 128
FRAMES = 8
KEEP = 2
SPOTS = 8
TOK_DEV = 64


EPS = 1e-06
NEG = -1e30


def from_behind(array, axis, by):
    devices = lax.axis_size(axis)
    pairs = [(i, i + by) for i in range(devices) if 0 <= i + by < devices]
    return lax.ppermute(array, axis, pairs)


def modulate(rows, shift, scale):
    values = rows.astype(jnp.float32)
    centre = values - jnp.mean(values, -1, keepdims=True)
    spread = jnp.mean(centre * centre, -1, keepdims=True)
    return (centre * lax.rsqrt(spread + EPS) * (1.0 + scale) + shift).astype(jnp.bfloat16)


def qk_scale(tensor, gain):
    square = jnp.mean(tensor * tensor, -1, keepdims=True)
    return (
        tensor * lax.rsqrt(square + EPS) * gain.reshape(tensor.shape[-2], tensor.shape[-1])
    ).astype(jnp.bfloat16)


def pick_level(table, level):
    matched = jnp.arange(table.shape[0]) == level
    picked = jnp.sum(jnp.where(matched[:, None, None], table, 0.0), 0)
    return (picked[0], picked[1], picked[2])


def lookup_one(table, index):
    matched = jnp.arange(table.shape[0], dtype=jnp.int32) == index
    return jnp.sum(jnp.where(matched, table, 0))


def fold_block(carry, query, block_keys, block_values, allow):
    best, total, acc = carry
    scores = jnp.einsum(
        "qhd,khd->hqk", query, block_keys, preferred_element_type=jnp.float32
    ) * HD ** (-0.5)
    scores = jnp.where(allow[None, None, :], scores, NEG)
    fresh = jnp.maximum(best, jnp.max(scores, -1))
    terms = jnp.where(allow[None, None, :], jnp.exp(scores - fresh[..., None]), 0.0)
    decay = jnp.exp(best - fresh)
    total = total * decay + jnp.sum(terms, -1)
    acc = acc * decay[..., None] + jnp.einsum(
        "hqk,khd->hqd", terms.astype(jnp.bfloat16), block_values, preferred_element_type=jnp.float32
    )
    return (fresh, total, acc)


def attention(proj, qk_gain, clip_id, visible_row, frame_counts):
    rows = proj.shape[0]
    cols = qk_gain.shape[1]
    heads = cols // HD
    tiles = rows // TOK_DEV
    lead = KEEP * SPOTS
    split = proj.reshape(rows, 3, heads, HD)
    query = qk_scale(split[:, 0], qk_gain[0])
    keys = qk_scale(split[:, 1], qk_gain[1])
    values = split[:, 2].astype(jnp.bfloat16)
    start_carry = (
        jnp.full((heads, rows), NEG, jnp.float32),
        jnp.zeros((heads, rows), jnp.float32),
        jnp.zeros((heads, rows, HD), jnp.float32),
    )
    everywhere = jnp.ones((rows,), jnp.bool_)
    own = fold_block(start_carry, query, keys, values, everywhere)
    lead_keys = keys.reshape(tiles, TOK_DEV, cols)[:, :lead].reshape(tiles * lead, cols)
    lead_values = values.reshape(tiles, TOK_DEV, cols)[:, :lead].reshape(tiles * lead, cols)
    packed = jnp.stack([lead_keys, lead_values], 0)[None]
    count = tiles * lead
    frame = jnp.arange(count, dtype=jnp.int32) % lead // SPOTS
    carry = own
    piece = lax.all_gather(packed, "span", axis=0, tiled=True)
    start = jnp.int32(0)
    for index in range(piece.shape[0]):
        source = start + index
        seen = lookup_one(visible_row, source)
        limit = lookup_one(frame_counts, source)
        allow = (frame < limit) & (source < clip_id) & (seen == 1)
        block_keys = piece[index, 0].reshape(count, heads, HD)
        block_values = piece[index, 1].reshape(count, heads, HD)
        carry = fold_block(carry, query, block_keys, block_values, allow)
    best, total, acc = carry
    return (acc / total[..., None]).transpose(1, 0, 2).reshape(rows, cols).astype(jnp.bfloat16)


def head_terms(attended, w_out):
    partial_term = jnp.dot(attended, w_out, preferred_element_type=jnp.float32).astype(jnp.bfloat16)
    return lax.optimization_barrier(partial_term).astype(jnp.float32)


def per_device(
    latents, levels, visible, frame_counts, modulation, w_qkv, qk_gain, w_out, w_head, conv_w
):
    current = latents[0]
    tok_rows = current.shape[0]
    width = current.shape[1]
    clip_id = lax.axis_index("span")
    level = levels[0]
    visible_row = lax.dynamic_index_in_dim(visible, clip_id, 0, keepdims=False)
    w_flat = w_qkv.reshape(width, -1)
    shift, scale, gate = pick_level(modulation, level)
    modulated = modulate(current, shift, scale)
    proj = jnp.dot(
        lax.all_gather(modulated, "tok", axis=0, tiled=True),
        w_flat,
        preferred_element_type=jnp.float32,
    )
    attended = attention(proj, qk_gain, clip_id, visible_row, frame_counts)
    summed = lax.psum_scatter(
        head_terms(attended, w_out).astype(jnp.bfloat16), "tok", scatter_dimension=0, tiled=True
    ).astype(jnp.float32)
    current = (current.astype(jnp.float32) + gate * summed).astype(jnp.bfloat16)
    channels = w_head.shape[1]
    feats = jnp.dot(current, w_head, preferred_element_type=jnp.float32).astype(jnp.bfloat16)
    feats = feats.reshape(FRAMES, tok_rows // FRAMES, channels)
    earlier = from_behind(feats[FRAMES - 2 :], "span", 1)
    sequence = jnp.concatenate([earlier, feats], 0)
    conv = jnp.zeros((tok_rows, conv_w.shape[2]), jnp.float32)
    for tap in range(3):
        window = sequence[2 - tap : 2 - tap + FRAMES].reshape(tok_rows, channels)
        conv = conv + jnp.dot(window, conv_w[tap], preferred_element_type=jnp.float32)
    decoded = jax.nn.silu(conv).astype(jnp.bfloat16)
    return (current[None], decoded[None])


def solution(mesh):
    placed = (
        P("span", "tok", None),
        P("span"),
        P(),
        P(),
        P(),
        P(None, None, "tok"),
        P(None, "tok"),
        P("tok", None),
        P(),
        P(),
    )
    return jax.shard_map(
        per_device,
        mesh=mesh,
        in_specs=placed,
        out_specs=(P("span", "tok", None), P("span", "tok", None)),
        check_vma=False,
    )
```

profile of v0, /device:TPU:0, one launch (start us, length us, event | category | flops | bytes accessed | tf_op | source)
XLA Modules:
  0.0 299.0 jit_solution(5046137200241144354)
XLA Ops:
  8.0 1.2 convert_reduce_fusion
  9.2 1.3 fusion.113
  10.5 1.3 select_reduce_fusion
  12.0 2.0 fusion.116
  14.1 8.3 %copy.78 = bf16[3584,3,256]{0,2,1:T(8,128)(2,1)} copy(bf16[3584,3,256]{2,0,1:T(8,128)(2,1)} %param.15) | data formatting | bytes 11010048 | tf_op args[5]
  23.0 62.1 %all-gather.4.cloned.1.call-done = bf16[1024,3584]{1,0:T(8,128)(2,1)} async-done(((bf16[64,3584]{1,0:T(8,128)(2,1)}), bf16[1024,3584]{1,0:T(8,128)(2,1)}) %all-gather.4.cloned.1.call-update) | async-done | bytes 7340048 | tf_op jit(solution)/shard_map/all_gather | solution.py:119
  85.1 9.8 %fusion = f32[1024,3,2,128]{0,3,2,1:T(8,128)S(1)} fusion(bf16[3,2,128,3584]{3,2,1,0:T(8,128)(2,1)} %bitcast.342, bf16[1024,3584]{1,0:T(8,128)(2,1)} %all-gather.4.cloned.1.call-done), kind=kOutput, calls=%fused_computation.3 | convolution fusion | flops 5637144576 | bytes 15990784 | tf_op jit(solution)/shard_map/dot_general | solution.py:118
  95.1 1.2 slice.205
  98.0 2.0 mul.275.clone
  100.0 3.1 %mul.283 = f32[16,64,256]{2,1,0:T(8,128)} reshape(f32[1024,2,128]{2,1,0:T(2,128)} %mul.275.clone) | data formatting | bytes 2097152 | tf_op jit(solution)/shard_map/mul | solution.py:33
  103.1 1.3 copy.84
  104.5 1.1 convert_element_type.88
  105.6 1.3 copy.82
  106.9 2.1 squeeze.31
  109.0 1.0 fusion.124
  110.1 0.7 pad_maximum_fusion
  110.9 1.5 fusion.169
  117.4 0.7 fusion.168
  118.2 1.3 and_and_fusion
  119.4 1.3 and_and_fusion.2
  120.8 1.2 and_and_fusion.4
  122.0 1.1 and_and_fusion.6
  123.2 1.4 multiply_convert_fusion
  124.6 5.8 %multiply_reduce_fusion = (f32[2,1024]{1,0:T(2,128)S(1)}, f32[2,1024,1024]{1,2,0:T(8,128)}) fusion(bf16[1024,2,128]{0,2,1:T(8,128)(2,1)S(1)} %multiply_convert_fusion, f32[2,128]{1,0:T(2,128)S(1)} %bitcast.365, f32[1024,2]{0,1:T(2,128)S(1)} %copy-done.6, f32[1024,3,2,128]{0,3,2,1:T(8,128)} %copy-done.1), kind=kOutput, calls=%fused_computation.1 | convolution fusion | flops 541849600 | bytes 9978880 | tf_op jit(solution)/shard_map/qhd,khd->hqk/dot_general | solution.py:50
  130.4 30.1 %all-gather.6.cloned.1.call-done = bf16[16,256,256]{2,1,0:T(8,128)(2,1)} async-done(((bf16[2,256,256]{2,1,0:T(8,128)(2,1)}), bf16[16,256,256]{2,1,0:T(8,128)(2,1)}) %all-gather.6.cloned.1.call-update) | async-done | bytes 2097168 | tf_op jit(solution)/shard_map/all_gather | solution.py:87
  160.5 3.9 %copy.85 = bf16[16,256,256]{1,2,0:T(8,128)(2,1)} copy(bf16[16,256,256]{2,1,0:T(8,128)(2,1)} %all-gather.6.cloned.1.call-done) | data formatting | bytes 4194304 | tf_op jit(solution)/shard_map/all_gather | solution.py:87
  164.4 1.7 fusion.202
  171.1 0.6 fusion.28
  171.8 0.6 fusion.26
  172.4 0.6 fusion.24
  173.7 0.6 fusion.20
  175.0 0.6 fusion.16
  175.6 1.4 fusion.2
  177.5 2.0 fusion.54
  179.5 0.7 fusion.50
  180.3 0.7 fusion.48
  181.0 0.7 fusion.46
  181.7 0.7 fusion.44
  182.5 0.7 fusion.42
  183.2 0.7 fusion.40
  184.0 0.7 fusion.38
  184.7 0.7 fusion.57
  185.5 5.1 %convolution_convert_fusion = bf16[1024,3584]{1,0:T(8,128)(2,1)} fusion(bf16[1024,256]{0,1:T(8,128)(2,1)S(1)} %bitcast.343, bf16[256,3584]{1,0:T(8,128)(2,1)S(1)} %copy-done), kind=kOutput, calls=%fused_computation.2 | convolution fusion | flops 1882718208 | bytes 9699328 | tf_op jit(solution)/shard_map/dot_general | solution.py:102
  190.6 94.9 %reduce-scatter.2.cloned.1.call-done = bf16[64,3584]{1,0:T(8,128)(2,1)} async-done(((bf16[1024,3584]{1,0:T(8,128)(2,1)}), bf16[64,3584]{1,0:T(8,128)(2,1)}) %reduce-scatter.2.cloned.1.call-update) | async-done | bytes 458768 | tf_op jit(solution)/shard_map/reduce_scatter | solution.py:124
  285.5 1.4 convolution_convert_fusion.1
  286.9 2.5 collective-permute-start
  289.5 1.9 fusion.126
  291.7 0.8 fusion.127
  (99 shorter events, 9.8 us)
Async XLA Ops:
  7.2 178.3 %copy-start = (bf16[256,3584]{1,0:T(8,128)(2,1)S(1)}, bf16[256,3584]{1,0:T(8,128)(2,1)}, u32[]{:S(2)}) copy-start(bf16[256,3584]{1,0:T(8,128)(2,1)} %param.17) | copy-start | bytes 5505028
  7.2 77.9 %all-gather.4.cloned.1.call-start = ((), (), s32[]{:S(2)}) async-start(), calls=%async_computation.1 | async-start | bytes 7798784 | tf_op jit(solution)/shard_map/all_gather | solution.py:119
  14.0 8.4 %copy-start.27 = (f32[2,256]{1,0:T(2,128)S(1)}, f32[2,256]{1,0:T(2,128)}, u32[]{:S(2)}) copy-start(f32[2,256]{1,0:T(2,128)} %param.16) | copy-start | bytes 6148
  14.0 146.5 %all-gather.6.cloned.1.call-start = ((), (), s32[]{:S(2)}) async-start(), calls=%async_computation.3 | async-start | bytes 2359296 | tf_op jit(solution)/shard_map/all_gather | solution.py:87
  94.8 1.9 copy-start.1
  97.4 0.6 copy-start.5
  100.0 5.6 %slice-start.2 = ((f32[1024,3,2,128]{0,3,2,1:T(8,128)}), f32[1024,1,2,128]{0,3,2,1:T(8,128)S(1)}, s32[]{:S(2)}) async-start(f32[1024,3,2,128]{0,3,2,1:T(8,128)} %copy-done.1), calls=%async_computation.6 | async-start | bytes 2097152 | tf_op jit(solution)/shard_map/slice | solution.py:72
  105.6 4.5 %slice-start.3 = ((bf16[16,64,256]{2,1,0:T(8,128)(2,1)}), bf16[16,16,256]{2,1,0:T(8,128)(2,1)S(1)}, s32[]{:S(2)}) async-start(bf16[16,64,256]{2,1,0:T(8,128)(2,1)} %convert_element_type.88), calls=%async_computation.7 | async-start | bytes 262144 | tf_op jit(solution)/shard_map/slice | solution.py:82
  106.9 2.1 copy-start.9
  106.9 10.5 %copy-start.28 = (s32[8]{0:T(128)S(1)}, s32[8]{0:T(128)}, u32[]{:S(2)}) copy-start(s32[8]{0:T(128)} %param.13) | copy-start | bytes 100
  106.9 16.2 %copy-start.8 = (f32[1024,2]{0,1:T(2,128)S(1)}, f32[1024,2]{0,1:T(2,128)}, u32[]{:S(2)}) copy-start(f32[1024,2]{0,1:T(2,128)} %get-tuple-element.81) | copy-start | bytes 24580
  106.9 16.3 %copy-start.26 = (f32[1,256]{1,0:T(1,128)S(1)}, f32[1,256]{1,0:T(1,128)}, u32[]{:S(2)}) copy-start(f32[1,256]{1,0:T(1,128)} %get-tuple-element.61) | copy-start | bytes 3076
  109.0 15.5 %copy-start.6 = (f32[1024,2]{0,1:T(2,128)S(1)}, f32[1024,2]{0,1:T(2,128)}, u32[]{:S(2)}) copy-start(f32[1024,2]{0,1:T(2,128)} %copy-done.5) | copy-start | bytes 24580
  110.8 174.7 %reduce-scatter.2.cloned.1.call-start = ((), (), s32[]{:S(2)}) async-start(), calls=%async_computation.2 | async-start | bytes 7798784 | tf_op jit(solution)/shard_map/reduce_scatter | solution.py:124
  119.4 51.1 %copy-start.10 = (pred[256]{0:T(512)(128)(4,1)}, pred[256]{0:T(512)(128)(4,1)S(1)}, u32[]{:S(2)}) copy-start(pred[256]{0:T(512)(128)(4,1)S(1)} %get-tuple-element.82) | copy-start | bytes 772
  119.4 51.7 %copy-start.12 = (pred[256]{0:T(512)(128)(4,1)}, pred[256]{0:T(512)(128)(4,1)S(1)}, u32[]{:S(2)}) copy-start(pred[256]{0:T(512)(128)(4,1)S(1)} %get-tuple-element.83) | copy-start | bytes 772
  120.8 51.0 %copy-start.14 = (pred[256]{0:T(512)(128)(4,1)}, pred[256]{0:T(512)(128)(4,1)S(1)}, u32[]{:S(2)}) copy-start(pred[256]{0:T(512)(128)(4,1)S(1)} %get-tuple-element.84) | copy-start | bytes 772
  120.8 51.6 %copy-start.16 = (pred[256]{0:T(512)(128)(4,1)}, pred[256]{0:T(512)(128)(4,1)S(1)}, u32[]{:S(2)}) copy-start(pred[256]{0:T(512)(128)(4,1)S(1)} %get-tuple-element.85) | copy-start | bytes 772
  122.0 46.3 %copy-start.18 = (pred[256]{0:T(512)(128)(4,1)}, pred[256]{0:T(512)(128)(4,1)S(1)}, u32[]{:S(2)}) copy-start(pred[256]{0:T(512)(128)(4,1)S(1)} %get-tuple-element.86) | copy-start | bytes 772
  122.0 46.8 %copy-start.20 = (pred[256]{0:T(512)(128)(4,1)}, pred[256]{0:T(512)(128)(4,1)S(1)}, u32[]{:S(2)}) copy-start(pred[256]{0:T(512)(128)(4,1)S(1)} %get-tuple-element.87) | copy-start | bytes 772
  123.1 46.2 %copy-start.22 = (pred[256]{0:T(512)(128)(4,1)}, pred[256]{0:T(512)(128)(4,1)S(1)}, u32[]{:S(2)}) copy-start(pred[256]{0:T(512)(128)(4,1)S(1)} %get-tuple-element.88) | copy-start | bytes 772
  123.2 46.7 %copy-start.24 = (pred[256]{0:T(512)(128)(4,1)}, pred[256]{0:T(512)(128)(4,1)S(1)}, u32[]{:S(2)}) copy-start(pred[256]{0:T(512)(128)(4,1)S(1)} %get-tuple-element.89) | copy-start | bytes 772
  170.5 5.1 %slice-start = ((s8[8388608]{0:T(1024)(128)(4,1)}), s8[4194304]{0:T(1024)(128)(4,1)S(1)}, s32[]{:S(2)}) async-start(s8[8388608]{0:T(1024)(128)(4,1)} %bitcast.339), calls=%async_computation.4 | async-start | bytes 8388608
  171.8 1.3 copy-start.19
  172.4 1.3 copy-start.21
  173.0 1.3 copy-start.23
  173.0 2.5 slice-start.1
  173.7 1.3 copy-start.25
  175.6 1.9 copy-start.2
  181.7 0.7 copy-start.17
  182.5 0.7 copy-start.15
  183.2 0.7 copy-start.13
  184.0 0.7 copy-start.11
  190.6 95.0 %copy-start.3 = (bf16[1,64,3584]{2,1,0:T(8,128)(2,1)S(1)}, bf16[1,64,3584]{2,1,0:T(8,128)(2,1)}, u32[]{:S(2)}) copy-start(bf16[1,64,3584]{2,1,0:T(8,128)(2,1)} %param.10) | copy-start | bytes 1376260
  190.6 95.0 %copy-start.4 = (bf16[3584,96]{0,1:T(8,128)(2,1)S(1)}, bf16[3584,96]{0,1:T(8,128)(2,1)}, u32[]{:S(2)}) copy-start(bf16[3584,96]{0,1:T(8,128)(2,1)} %param.18) | copy-start | bytes 2064388
  190.6 100.8 %copy-start.7 = (bf16[3,96,384]{2,1,0:T(8,128)(2,1)S(1)}, bf16[3,96,384]{2,1,0:T(8,128)(2,1)}, u32[]{:S(2)}) copy-start(bf16[3,96,384]{2,1,0:T(8,128)(2,1)} %param.19) | copy-start | bytes 663556
  286.9 4.6 %collective-permute-start = (bf16[2,8,96]{2,1,0:T(8,128)(2,1)S(1)}, bf16[2,8,96]{2,1,0:T(8,128)(2,1)S(1)}, u32[]{:S(2)}, u32[]{:S(2)}) collective-permute-start(bf16[2,8,96]{2,1,0:T(8,128)(2,1)S(1)} %slice_bitcast_fusion.1), channel_id=1, source_target_pairs={{0,16},{16,32},{32,48},{48,64},{64,80},{80,96},{96,112},{1,17},{17... | collective-permute-start | bytes 9224 | tf_op jit(solution)/shard_map/ppermute | solution.py:20
Sparse Core Ops, SparseCore 0:
  14.1 70.8 all-gather.3
  110.9 49.5 all-gather.5
  190.7 94.7 reduce-scatter.1
where the time goes:
time: 302 us; the launch traced here: 299 us
  waiting for transfers between devices  187 us (62%)
  matrix products  35.2 us (12%)
  local copies, waits for them, and re-layouts  28.4 us (9%)
  other arithmetic  25.5 us (8%)
  between operations  20.2 us (7%)
    reduce_scatter x1, waiting for transfers between devices, per_device(): lax.psum_scatter(head_terms(attended, w_out).astype(jnp.bfloat16), 'tok',...  94.9 us
    all_gather x1, waiting for transfers between devices, per_device(): lax.all_gather(modulated, 'tok', axis=0, tiled=True)  62.1 us
    all_gather x1, waiting for transfers between devices, attention(): piece = lax.all_gather(packed, 'span', axis=0, tiled=True)  30.1 us
    dot_general x9, matrix products, fold_block(): jnp.einsum('qhd,khd->hqk', query, block_keys, preferred_element_type=jnp....  9.98 us
    unnamed x64, local copies, waits for them, and re-layouts  9.9 us
    dot_general x1, matrix products, per_device(): jnp.dot(lax.all_gather(modulated, 'tok', axis=0, tiled=True), w_flat, pre...  9.76 us
    dot_general x9, matrix products, fold_block(): jnp.einsum('hqk,khd->hqd', terms.astype(jnp.bfloat16), block_values, pref...  7.87 us
    reduce_sum x9, other arithmetic, fold_block(): total = total * decay + jnp.sum(terms, -1)  6.35 us
  transfers between devices with their start and end apart: 4, of which 3 were waited for; matrix products, arithmetic and copies ran while one was open for 8% of the time, Pallas kernels for 0%

commit v1 on v0

v1 whole, which is shorter than its diff:
```python
import jax
import jax.numpy as jnp
from jax import lax
from jax.experimental import pallas as pl
from jax.experimental.pallas import tpu as pltpu
from jax.sharding import PartitionSpec as P

HD = 128
FRAMES = 8
KEEP = 2
SPOTS = 8
TOK_DEV = 64
EPS = 1e-06
LOG2E = 1.4426950408889634

MESH = pl.DeviceIdType.MESH
F32 = jnp.float32
BF16 = jnp.bfloat16

OWN, DOWN, UP, FAR, ACROSS, XDOWN, XUP, XFAR = range(8)
HALF = TOK_DEV // 2


def places():
    s = lax.axis_index("span")
    t = lax.axis_index("tok")
    z, yh, c = t // 4, (t // 2) % 2, t % 2
    x, yl = s // 2, s % 2

    def tok(z, yh, c):
        return z * 4 + yh * 2 + c

    return dict(
        s=s,
        up=(s, tok((z + 1) % 4, yh, c)),
        down=(s, tok((z + 3) % 4, yh, c)),
        across=(s, tok(z, 1 - yh, c)),
        twin=(s, tok(z, yh, 1 - c)),
        right=(((x + 1) % 4) * 2 + yl, t),
        left=(((x + 3) % 4) * 2 + yl, t),
        pair=(x * 2 + 1 - yl, t),
        after=((s + 1) % 8, t),
        before=((s + 7) % 8, t),
    )


def greet(at, names):
    barrier = pltpu.get_barrier_semaphore()
    for name in names:
        pl.semaphore_signal(barrier, inc=1, device_id=at[name], device_id_type=MESH)
    return lambda: pl.semaphore_wait(barrier, len(names))


class Post:
    def __init__(self, send, recv):
        self.send, self.recv, self.copies = send, recv, []

    def __call__(self, src, dst, device):
        index = len(self.copies)
        copy = pltpu.make_async_remote_copy(
            src_ref=src,
            dst_ref=dst,
            send_sem=self.send.at[index],
            recv_sem=self.recv.at[index],
            device_id=device,
            device_id_type=MESH,
        )
        copy.start()
        self.copies.append(copy)
        return copy

    def drain(self):
        for copy in self.copies:
            copy.wait_send()


GATHER_COPIES = 30 + 42 + 1
GROUPS = ((0, 128), (128, 256), (384, 256), (640, 256), (896, 128))


def gather_kernel(
    levels, lat, mod, wqkv, gain, wout,
    q_out, k_out, v_out, kv_out, wtwin,
    xbuf, wbuf, kvbuf, send, recv, local,
):
    at = places()
    peers = ("twin", "up", "down", "across", "right", "left", "pair")
    met = greet(at, peers)
    loads = [pltpu.make_async_copy(wqkv.at[j], wbuf.at[j], local.at[j]) for j in range(3)]
    for load in loads:
        load.start()
    level = levels[0]
    shift = mod[0, pl.ds(level, 1), :]
    scale = 1.0 + mod[1, pl.ds(level, 1), :]
    for row in range(0, TOK_DEV, 16):
        values = lat[row : row + 16, :].astype(F32)
        centre = values - jnp.mean(values, -1, keepdims=True)
        spread = jnp.mean(centre * centre, -1, keepdims=True)
        xbuf[row : row + 16, :] = (centre * lax.rsqrt(spread + EPS) * scale + shift).astype(BF16)
    met()
    post = Post(send, recv)

    def part(place, core, half):
        return xbuf.at[pl.ds((place * 2 + core) * TOK_DEV + half * HALF, HALF)]

    def hand(place, half, core=1):
        return post(part(place, 0, half), part(place, core, half), at["twin"])

    def move(source, target, half, to):
        return post(part(source, 0, half), part(target, 0, half), at[to])

    up, down, across, twin = {}, {}, {}, {}
    for first in (0, 1):
        up[first] = move(OWN, DOWN, first, "up")
        down[1 - first] = move(OWN, UP, 1 - first, "down")
        across[first] = move(OWN, ACROSS, first, "across")
        twin[OWN, first] = hand(OWN, first)
    weights = post(wout, wtwin, at["twin"])

    def project(group):
        start, rows = GROUPS[group]
        tiles = rows // TOK_DEV
        x = xbuf[start : start + rows, :]
        for j, out in enumerate((q_out, k_out, v_out)):
            p = jnp.dot(x, wbuf[j], preferred_element_type=F32)
            if j < 2:
                heads = []
                for h in range(2):
                    t = p[:, h * HD : (h + 1) * HD]
                    square = jnp.mean(t * t, -1, keepdims=True)
                    g = gain[j : j + 1, h * HD : (h + 1) * HD]
                    if j == 0:
                        g = g * (LOG2E * HD ** (-0.5))
                    heads.append(t * lax.rsqrt(square + EPS) * g)
                p = jnp.concatenate(heads, -1)
            out[start : start + rows, :] = p.astype(BF16)
            if j > 0:
                lead = p.reshape(tiles, FRAMES, SPOTS, 2 * HD)
                for f in range(KEEP):
                    kvbuf[0, f, start // 8 : (start + rows) // 8, (j - 1) * 256 : j * 256] = (
                        lead[:, f].reshape(tiles * SPOTS, 2 * HD).astype(BF16)
                    )

    ranges = ((0, 80), (80, 32), (112, 16))

    class Spread:
        def __init__(self, index):
            self.first, self.rows = ranges[index]

        def move(self, source, target, f, to):
            rows = pl.ds(self.first, self.rows)
            return post(kvbuf.at[source, f, rows], kvbuf.at[target, f, rows], at[to])

        def begin(self):
            self.right = [self.move(0, 1, f, "right") for f in range(2)]
            self.left = [self.move(0, 3, f, "left") for f in range(2)]
            self.pair = [self.move(0, 4, f, "pair") for f in range(2)]

        def second(self):
            self.right[0].wait_recv()
            self.far = [self.move(1, 2, 0, "right")]
            self.left[1].wait_recv()
            self.far.append(self.move(3, 2, 1, "left"))
            self.over_right, self.over_left = [], []
            for f in range(2):
                self.pair[f].wait_recv()
                self.over_right.append(self.move(4, 5, f, "right"))
                self.over_left.append(self.move(4, 7, f, "left"))
            self.right[1].wait_recv()
            self.left[0].wait_recv()

        def third(self):
            self.over_right[0].wait_recv()
            self.far.append(self.move(5, 6, 0, "right"))
            self.over_left[1].wait_recv()
            self.far.append(self.move(7, 6, 1, "left"))
            self.over_right[1].wait_recv()
            self.over_left[0].wait_recv()

        def end(self):
            for copy in self.far:
                copy.wait_recv()

    spread = [Spread(index) for index in range(3)]

    for half in range(2):
        twin[OWN, half].wait_recv()
    for load in loads:
        load.wait()
    project(0)

    far, over_up, over_down, over_far = {}, {}, {}, {}
    up[0].wait_recv()
    far[0] = move(DOWN, FAR, 0, "up")
    twin[DOWN, 0] = hand(DOWN, 0)
    down[1].wait_recv()
    far[1] = move(UP, FAR, 1, "down")
    twin[UP, 1] = hand(UP, 1)
    up[1].wait_recv()
    twin[DOWN, 1] = hand(DOWN, 1)
    down[0].wait_recv()
    twin[UP, 0] = hand(UP, 0)
    across[0].wait_recv()
    over_up[0] = move(ACROSS, XDOWN, 0, "up")
    over_down[0] = move(ACROSS, XUP, 0, "down")
    twin[ACROSS, 0] = hand(ACROSS, 0)
    for place in (DOWN, UP):
        for half in range(2):
            twin[place, half].wait_recv()
    project(1)

    for half in range(2):
        far[half].wait_recv()
        twin[FAR, half] = hand(FAR, half)
    across[1].wait_recv()
    over_up[1] = move(ACROSS, XDOWN, 1, "up")
    over_down[1] = move(ACROSS, XUP, 1, "down")
    twin[ACROSS, 1] = hand(ACROSS, 1)
    for place in (FAR, ACROSS):
        for half in range(2):
            twin[place, half].wait_recv()
    project(2)
    spread[0].begin()

    over_up[0].wait_recv()
    over_far[0] = move(XDOWN, XFAR, 0, "up")
    twin[XDOWN, 0] = hand(XDOWN, 0)
    over_down[0].wait_recv()
    twin[XUP, 0] = hand(XUP, 0)
    over_down[1].wait_recv()
    over_far[1] = move(XUP, XFAR, 1, "down")
    twin[XUP, 1] = hand(XUP, 1)
    over_up[1].wait_recv()
    twin[XDOWN, 1] = hand(XDOWN, 1)
    spread[0].second()
    for place in (XDOWN, XUP):
        for half in range(2):
            twin[place, half].wait_recv()
    project(3)
    spread[1].begin()

    for half in range(2):
        over_far[half].wait_recv()
        twin[XFAR, half] = hand(XFAR, half)
    spread[0].third()
    for half in range(2):
        twin[XFAR, half].wait_recv()
    project(4)
    spread[2].begin()
    spread[1].second()
    spread[2].second()
    spread[1].third()
    spread[2].third()
    for item in spread:
        item.end()
    keep = pltpu.make_async_copy(kvbuf.at[pl.ds(1, 7)], kv_out, local.at[3])
    keep.start()
    weights.wait_recv()
    post.drain()
    keep.wait()
    assert len(post.copies) == GATHER_COPIES


def gather(levels, lat, mod, wqkv, gain, wout):
    rows, width = 16 * TOK_DEV, lat.shape[1]
    vmem = pl.BlockSpec(memory_space=pltpu.VMEM)
    anywhere = pl.BlockSpec(memory_space=pl.ANY)
    tensor = jax.ShapeDtypeStruct((rows, 2 * HD), BF16)
    return pl.pallas_call(
        gather_kernel,
        out_shape=(
            tensor, tensor, tensor,
            jax.ShapeDtypeStruct((7, KEEP, 128, 512), BF16),
            jax.ShapeDtypeStruct(wout.shape, BF16),
        ),
        in_specs=[pl.BlockSpec(memory_space=pltpu.SMEM), vmem, vmem, anywhere, vmem, anywhere],
        out_specs=(vmem, vmem, vmem, anywhere, anywhere),
        scratch_shapes=[
            pltpu.VMEM((rows, width), BF16),
            pltpu.VMEM((3, width, 2 * HD), BF16),
            pltpu.VMEM((8, KEEP, 128, 512), BF16),
            pltpu.SemaphoreType.DMA((GATHER_COPIES,)),
            pltpu.SemaphoreType.DMA((GATHER_COPIES,)),
            pltpu.SemaphoreType.DMA((4,)),
        ],
        compiler_params=pltpu.CompilerParams(
            collective_id=0, has_side_effects=True, vmem_limit_bytes=44 * 2**20
        ),
        name="gather_project",
    )(levels, lat, mod, wqkv, gain, wout)


def attend_kernel(visible, counts, q, k, v, kv, out, best, total, acc):
    s = lax.axis_index("span")
    x, yl = s // 2, s % 2
    contract = (((1,), (1,)), ((), ()))
    for h in range(2):
        cols = slice(h * HD, (h + 1) * HD)
        scores = lax.dot_general(q[:, cols], k[:, cols], contract, preferred_element_type=F32)
        top = jnp.max(scores, -1, keepdims=True)
        terms = jnp.exp2(scores - top)
        best[h] = top
        total[h] = jnp.sum(terms, -1, keepdims=True)
        acc[h] = jnp.dot(terms.astype(BF16), v[:, cols], preferred_element_type=F32)

    def fold(keys, values):
        for h in range(2):
            cols = slice(h * HD, (h + 1) * HD)
            scores = lax.dot_general(
                q[:, cols], keys[:, cols], contract, preferred_element_type=F32
            )
            old = best[h]
            fresh = jnp.maximum(old, jnp.max(scores, -1, keepdims=True))
            terms = jnp.exp2(scores - fresh)
            decay = jnp.exp2(old - fresh)
            best[h] = fresh
            total[h] = total[h] * decay + jnp.sum(terms, -1, keepdims=True)
            acc[h] = acc[h] * decay + jnp.dot(
                terms.astype(BF16), values[:, cols], preferred_element_type=F32
            )

    def one(index, carry):
        place = index + 1
        source = ((x + 4 - place % 4) % 4) * 2 + (yl + place // 4) % 2
        seen = (source < s) & (visible[s, source] == 1)
        count = counts[source]

        @pl.when(seen & (count >= 2))
        def _():
            both = kv[index].reshape(2 * 128, 512)
            fold(both[:, :256], both[:, 256:])

        @pl.when(seen & (count == 1))
        def _():
            lead = kv[index, 0]
            fold(lead[:, :256], lead[:, 256:])

        return carry

    lax.fori_loop(0, 7, one, 0)
    for h in range(2):
        out[:, h * HD : (h + 1) * HD] = (acc[h] / total[h]).astype(BF16)


def attend(visible, counts, q, k, v, kv):
    rows = q.shape[0]
    block = 256
    smem = pl.BlockSpec(memory_space=pltpu.SMEM)
    whole = pl.BlockSpec((rows, 2 * HD), lambda i: (0, 0))
    tile = pl.BlockSpec((block, 2 * HD), lambda i: (i, 0))
    return pl.pallas_call(
        attend_kernel,
        grid=(rows // block,),
        out_shape=jax.ShapeDtypeStruct((rows, 2 * HD), BF16),
        in_specs=[
            smem, smem, tile, whole, whole,
            pl.BlockSpec((7, KEEP, 128, 512), lambda i: (0, 0, 0, 0)),
        ],
        out_specs=tile,
        scratch_shapes=[
            pltpu.VMEM((2, block, 1), F32),
            pltpu.VMEM((2, block, 1), F32),
            pltpu.VMEM((2, block, HD), F32),
        ],
        compiler_params=pltpu.CompilerParams(vmem_limit_bytes=40 * 2**20),
        name="attend",
    )(visible, counts, q, k, v, kv)


REDUCE_COPIES = 16


def reduce_kernel(
    levels, att, wout, wtwin, lat, mod, whead, conv_w,
    den, dec,
    wbuf, atwin, partial, outbox, farbox, zbox, ybox, heads, taps, tail, halo,
    send, recv, local,
):
    at = places()
    peers = ("twin", "up", "down", "across", "after", "before")
    met = greet(at, peers)
    width = lat.shape[1]
    depth = wout.shape[0]
    loads = [
        pltpu.make_async_copy(wout, wbuf.at[pl.ds(0, depth)], local.at[0]),
        pltpu.make_async_copy(wtwin, wbuf.at[pl.ds(depth, depth)], local.at[1]),
    ]
    for load in loads:
        load.start()
    met()
    post = Post(send, recv)
    shared = post(att.at[:, 1], atwin, at["twin"])
    heads[96:, :] = jnp.zeros((32, width), BF16)
    heads[:96, :] = whead[...]
    taps[:, 96:, :] = jnp.zeros((3, 32, taps.shape[2]), BF16)
    taps[:, :96, :] = conv_w[...]
    for load in loads:
        load.wait()
    shared.wait_recv()
    tile = 512

    def multiply(spots):
        a = jnp.concatenate(
            [jnp.concatenate([att[p, 0], atwin[p]], -1) for p in spots], 0
        )
        for col in range(0, width, tile):
            r = jnp.dot(a, wbuf[:, col : col + tile], preferred_element_type=F32)
            for i, p in enumerate(spots):
                partial[p, :, col : col + tile] = r[i * TOK_DEV : (i + 1) * TOK_DEV]

    def rows(half):
        return slice(half * HALF, (half + 1) * HALF)

    def ship(spot, half, box, to, *added):
        value = partial[spot, rows(half), :]
        for other in added:
            value = value + other[rows(half), :].astype(F32)
        outbox[spot, rows(half), :] = value.astype(BF16)
        piece = pl.ds(half * HALF, HALF)
        return post(outbox.at[spot, piece], box.at[piece], at[to])


    multiply((XFAR,))
    far_up = ship(XFAR, 0, farbox.at[1], "up")
    far_down = ship(XFAR, 1, farbox.at[1], "down")
    multiply((XDOWN, XUP))
    down, up = {}, {}
    down[1, 0] = ship(XDOWN, 0, zbox.at[1, 1], "down")
    multiply((FAR,))
    far_up.wait_recv()
    up[1, 0] = ship(XUP, 0, zbox.at[1, 0], "up", farbox.at[1])
    up[1, 1] = ship(XUP, 1, zbox.at[1, 0], "up")
    far_down.wait_recv()
    down[1, 1] = ship(XDOWN, 1, zbox.at[1, 1], "down", farbox.at[1])
    far_up = ship(FAR, 0, farbox.at[0], "up")
    far_down = ship(FAR, 1, farbox.at[0], "down")
    multiply((DOWN, UP))
    up[0, 1] = ship(UP, 1, zbox.at[0, 0], "up")
    down[0, 0] = ship(DOWN, 0, zbox.at[0, 1], "down")
    multiply((ACROSS, OWN))
    over = {}
    for half in range(2):
        up[1, half].wait_recv()
        down[1, half].wait_recv()
        over[half] = ship(ACROSS, half, ybox, "across", zbox.at[1, 0], zbox.at[1, 1])
    far_up.wait_recv()
    up[0, 0] = ship(UP, 0, zbox.at[0, 0], "up", farbox.at[0])
    far_down.wait_recv()
    down[0, 1] = ship(DOWN, 1, zbox.at[0, 1], "down", farbox.at[0])

    gate = mod[2, pl.ds(levels[0], 1), :]
    for half in (1, 0):
        up[0, half].wait_recv()
        down[0, half].wait_recv()
        if half == 1:
            continue
        over[0].wait_recv()
        over[1].wait_recv()
    for row in range(0, TOK_DEV, 16):
        piece = slice(row, row + 16)
        mixed = partial[OWN, piece, :]
        for box in (zbox.at[0, 0], zbox.at[0, 1], ybox):
            mixed = mixed + box[piece, :].astype(F32)
        den[piece, :] = (lat[piece, :].astype(F32) + gate * mixed).astype(BF16)
    feats = lax.dot_general(
        den[...], heads[...], (((1,), (1,)), ((), ())), preferred_element_type=F32
    ).astype(BF16).astype(F32)
    tail[...] = feats[TOK_DEV - 2 * SPOTS :].astype(BF16)
    edge = post(tail, halo, at["after"])
    edge.wait_recv()
    earlier = jnp.where(at["s"] > 0, halo[...].astype(F32), 0.0)
    sequence = jnp.concatenate([earlier, feats], 0)
    conv = jnp.zeros(dec.shape, F32)
    for tap in range(3):
        begin = (2 - tap) * SPOTS
        window = sequence[begin : begin + TOK_DEV].astype(BF16)
        conv = conv + jnp.dot(window, taps[tap], preferred_element_type=F32)
    dec[...] = (conv / (1.0 + jnp.exp(-conv))).astype(BF16)
    post.drain()
    assert len(post.copies) == REDUCE_COPIES


def reduce(levels, att, wout, wtwin, lat, mod, whead, conv_w):
    width, depth = lat.shape[1], wout.shape[0]
    vmem = pl.BlockSpec(memory_space=pltpu.VMEM)
    anywhere = pl.BlockSpec(memory_space=pl.ANY)
    return pl.pallas_call(
        reduce_kernel,
        out_shape=(
            jax.ShapeDtypeStruct(lat.shape, BF16),
            jax.ShapeDtypeStruct((lat.shape[0], conv_w.shape[2]), BF16),
        ),
        in_specs=[
            pl.BlockSpec(memory_space=pltpu.SMEM), vmem, anywhere, anywhere, vmem, vmem, vmem, vmem,
        ],
        out_specs=(vmem, vmem),
        scratch_shapes=[
            pltpu.VMEM((2 * depth, width), BF16),
            pltpu.VMEM((8, TOK_DEV, 2 * HD), BF16),
            pltpu.VMEM((8, TOK_DEV, width), F32),
            pltpu.VMEM((8, TOK_DEV, width), BF16),
            pltpu.VMEM((2, TOK_DEV, width), BF16),
            pltpu.VMEM((2, 2, TOK_DEV, width), BF16),
            pltpu.VMEM((TOK_DEV, width), BF16),
            pltpu.VMEM((128, width), BF16),
            pltpu.VMEM((3, 128, conv_w.shape[2]), BF16),
            pltpu.VMEM((2 * SPOTS, 128), BF16),
            pltpu.VMEM((2 * SPOTS, 128), BF16),
            pltpu.SemaphoreType.DMA((REDUCE_COPIES,)),
            pltpu.SemaphoreType.DMA((REDUCE_COPIES,)),
            pltpu.SemaphoreType.DMA((2,)),
        ],
        compiler_params=pltpu.CompilerParams(
            collective_id=1, has_side_effects=True, vmem_limit_bytes=44 * 2**20
        ),
        name="reduce_decode",
    )(levels, att, wout, wtwin, lat, mod, whead, conv_w)


def per_device(
    latents, levels, visible, frame_counts, modulation, w_qkv, qk_gain, w_out, w_head, conv_w
):
    lat = latents[0]
    mod = modulation.transpose(1, 0, 2)
    query, keys, values, lead, wtwin = gather(
        levels, lat, mod, w_qkv.transpose(1, 0, 2), qk_gain, w_out
    )
    attended = attend(visible, frame_counts, query, keys, values, lead)
    attended = attended.reshape(8, 2, TOK_DEV, 2 * HD)
    denoised, decoded = reduce(levels, attended, w_out, wtwin, lat, mod, w_head.T, conv_w)
    return (denoised[None], decoded[None])


def solution(mesh):
    placed = (
        P("span", "tok", None),
        P("span"),
        P(),
        P(),
        P(),
        P(None, None, "tok"),
        P(None, "tok"),
        P("tok", None),
        P(),
        P(),
    )
    return jax.shard_map(
        per_device,
        mesh=mesh,
        in_specs=placed,
        out_specs=(P("span", "tok", None), P("span", "tok", None)),
        check_vma=False,
    )
```

time: 302 us -> 123 us (0.41)
  waiting for transfers between devices: 187 us -> 0 us
  Pallas kernels: 0 us -> 115 us
  matrix products: 35.2 us -> 0 us
  other arithmetic: 25.5 us -> 0 us
  local copies, waits for them, and re-layouts: 28.4 us -> 5.71 us
  between operations: 20.2 us -> 1.38 us
    pallas_call x0 -> x3, Pallas kernels: none -> 115 us  [the longest x1 54.5 us: reduce(): pl.pallas_call(reduce_kernel, out_shape=(jax.ShapeDtypeStruct(lat.shape,...]
    reduce_scatter x1 -> x0, waiting for transfers between devices: 94.9 us -> none  [per_device(): lax.psum_scatter(head_terms(attended, w_out).astype(jnp.bfloat16), 'tok',...]
    all_gather x2 -> x0, waiting for transfers between devices: 92.2 us -> none  [the longest x1 62.1 us: per_device(): lax.all_gather(modulated, 'tok', axis=0, tiled=True)]
    dot_general x24 -> x0, matrix products: 35.2 us -> none  [the longest x9 9.98 us: fold_block(): jnp.einsum('qhd,khd->hqk', query, block_keys, preferred_element_type=jnp....]
    reduce_sum x15 -> x0, other arithmetic: 12.7 us -> none  [the longest x9 6.35 us: fold_block(): total = total * decay + jnp.sum(terms, -1)]
    mul x2 -> x0, local copies, waits for them, and re-layouts: 5.16 us -> none  [qk_scale(): tensor * lax.rsqrt(square + EPS)]
    and x4 -> x0, other arithmetic: 4.9 us -> none  [attention(): allow = (frame < limit) & (source < clip_id) & (seen == 1)]
    slice x9 -> x0, local copies, waits for them, and re-layouts: 4.89 us -> none  [the longest x4 1.93 us: attention(): keys = qk_scale(split[:, 1], qk_gain[1])]
  transfers between devices with their start and end apart: 4 -> 0, of which waited for: 3 -> 0; matrix products, arithmetic and copies ran while one was open for 8% -> 0% of each run, Pallas kernels for 0% -> 0%
where the time goes in v1:
time: 123 us; the launch traced here: 122 us
  Pallas kernels  115 us (93%)
  local copies, waits for them, and re-layouts  5.71 us (5%)
  between operations  1.38 us (1%)
    pallas_call x1, Pallas kernels, reduce(): pl.pallas_call(reduce_kernel, out_shape=(jax.ShapeDtypeStruct(lat.shape,...  54.5 us
    pallas_call x1, Pallas kernels, gather(): pl.pallas_call(gather_kernel, out_shape=(tensor, tensor, tensor, jax.Shap...  54.2 us
    pallas_call x1, Pallas kernels, attend(): pl.pallas_call(attend_kernel, grid=(rows // block,), out_shape=jax.ShapeD...  6.65 us
    unnamed x20, local copies, waits for them, and re-layouts  5.71 us

profile of v1, /device:TPU:0, one launch (start us, length us, event | category | flops | bytes accessed | tf_op | source)
XLA Modules:
  0.0 122.4 jit_solution(14588484532023503938)
XLA Ops:
  1.3 0.0 copy-start
  1.3 1.5 %copy-done = bf16[256,3584]{1,0:T(8,128)(2,1)S(1)} copy-done((bf16[256,3584]{1,0:T(8,128)(2,1)S(1)}, bf16[256,3584]{1,0:T(8,128)(2,1)}, u32[]{:S(2)}) %copy-start) | copy-done | bytes 1835032
  2.8 0.0 copy-start.2
  2.8 1.1 copy-done.2
  3.9 0.0 copy-start.3
  3.9 1.0 copy-done.3
  4.9 0.0 copy-start.7
  4.9 0.7 copy-done.7
  5.6 0.0 copy-start.6
  5.6 0.0 copy-start.8
  5.6 54.2 %gather_project.1 = (bf16[1024,256]{1,0:T(8,128)(2,1)S(1)}, bf16[1024,256]{1,0:T(8,128)(2,1)S(1)}, bf16[1024,256]{1,0:T(8,128)(2,1)S(1)}, bf16[7,2,128,512]{3,2,1,0:T(8,128)(2,1)S(1)}, bf16[256,3584]{1,0:T(8,128)(2,1)S(1)}) custom-call(s32[1]{0:T(128)S(6)} %copy.14.levels, bf16[64,3584]{1,0:T(8,128)(2,1)S(1)} %bitcast.10, f32[3,16,3584]{2,1,0:T(8,128)S(1)} %bitcast.7, ...), custom_call_target="tpu_custom_call" | custom-call | tf_op jit(solution)/shard_map/gather_project/pallas_call | solution.py:269
  59.7 0.0 copy-done.6
  59.8 0.0 copy-done.8
  59.8 0.0 copy-start.1
  59.8 0.0 copy-start.4
  59.8 0.0 copy-start.5
  59.8 6.6 %attend.1 = bf16[1024,256]{1,0:T(8,128)(2,1)S(1)} custom-call(s32[8,8]{1,0:T(8,128)S(1)} %copy-done.6, s32[8]{0:T(128)S(1)} %copy-done.8, bf16[1024,256]{1,0:T(8,128)(2,1)S(1)} %get-tuple-element.9.q, bf16[1024,256]{1,0:T(8,128)(2,1)S(1)} %get-tuple-element.10.k, bf16[1024,256]{1,0:T(8,128)(2,1)S(1)} %get-tuple-element.11.v, ...), custom_call_target="tpu_custom_call" | custom-call | tf_op jit(solution)/shard_map/attend/pallas_call | solution.py:351
  66.5 0.0 copy-done.1
  66.5 0.0 copy-done.4
  66.5 0.0 copy-done.5
  66.5 54.5 %reduce_decode.1 = (bf16[64,3584]{1,0:T(8,128)(2,1)S(1)}, bf16[64,384]{1,0:T(8,128)(2,1)S(1)}) custom-call(s32[1]{0:T(128)S(6)} %copy.14.levels, bf16[8,2,64,256]{3,2,1,0:T(8,128)(2,1)S(1)} %bitcast.9, bf16[256,3584]{1,0:T(8,128)(2,1)S(1)} %copy-done.1, bf16[256,3584]{1,0:T(8,128)(2,1)S(1)} %get-tuple-element.13.wtwin, bf16[64,3584]{1,0:T(8,128)(2,1)S(1)} %bitcast.11, ...), custom_call_target="tpu_custom_call" | custom-call | tf_op jit(solution)/shard_map/reduce_decode/pallas_call | solution.py:487
  121.0 0.8 copy.15
  121.8 0.6 copy.16
Async XLA Ops:
  1.3 1.5 %copy-start = (bf16[256,3584]{1,0:T(8,128)(2,1)S(1)}, bf16[256,3584]{1,0:T(8,128)(2,1)}, u32[]{:S(2)}) copy-start(bf16[256,3584]{1,0:T(8,128)(2,1)} %wout.3) | copy-start | bytes 5505028
  2.8 1.1 copy-start.2
  3.9 1.0 copy-start.3
  4.9 0.7 copy-start.7
  5.6 54.2 %copy-start.6 = (s32[8,8]{1,0:T(8,128)S(1)}, s32[8,8]{1,0:T(8,128)}, u32[]{:S(2)}) copy-start(s32[8,8]{1,0:T(8,128)} %visible.1) | copy-start | bytes 772
  5.6 54.2 %copy-start.8 = (s32[8]{0:T(128)S(1)}, s32[8]{0:T(128)}, u32[]{:S(2)}) copy-start(s32[8]{0:T(128)} %counts.1) | copy-start | bytes 100
  59.8 6.7 %copy-start.1 = (bf16[256,3584]{1,0:T(8,128)(2,1)S(1)}, bf16[256,3584]{1,0:T(8,128)(2,1)}, u32[]{:S(2)}) copy-start(bf16[256,3584]{1,0:T(8,128)(2,1)} %wout.3) | copy-start | bytes 5505028
  59.8 6.7 %copy-start.4 = (bf16[3584,96]{0,1:T(8,128)(2,1)S(1)}, bf16[3584,96]{0,1:T(8,128)(2,1)}, u32[]{:S(2)}) copy-start(bf16[3584,96]{0,1:T(8,128)(2,1)} %param.18) | copy-start | bytes 2064388
  59.8 6.7 %copy-start.5 = (bf16[3,96,384]{2,1,0:T(8,128)(2,1)S(1)}, bf16[3,96,384]{2,1,0:T(8,128)(2,1)}, u32[]{:S(2)}) copy-start(bf16[3,96,384]{2,1,0:T(8,128)(2,1)} %conv_w.1) | copy-start | bytes 663556

commit v2 on v1

v2 whole, which is shorter than its diff:
```python
import jax
import jax.numpy as jnp
from jax import lax
from jax.experimental import pallas as pl
from jax.experimental.pallas import tpu as pltpu
from jax.sharding import PartitionSpec as P

HD = 128
FRAMES = 8
KEEP = 2
SPOTS = 8
TOK_DEV = 64
EPS = 1e-06
LOG2E = 1.4426950408889634

MESH = pl.DeviceIdType.MESH
F32 = jnp.float32
BF16 = jnp.bfloat16

OWN, DOWN, UP, FAR, ACROSS, XDOWN, XUP, XFAR = range(8)
HALF = TOK_DEV // 2


def places():
    s = lax.axis_index("span")
    t = lax.axis_index("tok")
    z, yh, c = t // 4, (t // 2) % 2, t % 2
    x, yl = s // 2, s % 2

    def tok(z, yh, c):
        return z * 4 + yh * 2 + c

    return dict(
        s=s,
        up=(s, tok((z + 1) % 4, yh, c)),
        down=(s, tok((z + 3) % 4, yh, c)),
        across=(s, tok(z, 1 - yh, c)),
        twin=(s, tok(z, yh, 1 - c)),
        right=(((x + 1) % 4) * 2 + yl, t),
        left=(((x + 3) % 4) * 2 + yl, t),
        pair=(x * 2 + 1 - yl, t),
        after=((s + 1) % 8, t),
        before=((s + 7) % 8, t),
    )


def greet(at, names):
    barrier = pltpu.get_barrier_semaphore()
    for name in names:
        pl.semaphore_signal(barrier, inc=1, device_id=at[name], device_id_type=MESH)
    return lambda: pl.semaphore_wait(barrier, len(names))


class Post:
    def __init__(self, send, recv):
        self.send, self.recv, self.copies = send, recv, []

    def __call__(self, src, dst, device):
        index = len(self.copies)
        copy = pltpu.make_async_remote_copy(
            src_ref=src,
            dst_ref=dst,
            send_sem=self.send.at[index],
            recv_sem=self.recv.at[index],
            device_id=device,
            device_id_type=MESH,
        )
        copy.start()
        self.copies.append(copy)
        return copy

    def drain(self):
        for copy in self.copies:
            copy.wait_send()

COPIES = 30 + 56 + 1 + 8 + 14 + 1
GROUPS = ((0, 128), (128, 256), (384, 256), (640, 256), (896, 128))
PENALTY = 1e30
WIDE = 2 * HD


def layer_kernel(
    levels, visible, counts, lat_in, mod_in, wqkv, gain_in, wout, whead, conv_w,
    den, dec,
    lat, mod, gain, xbuf, wbuf, qbuf, kbuf, vbuf, kvbuf, best, total, acc, att, atwin,
    obuf, partial, outbox, fx, cx, fo, yx, zd, zu, ya, heads, taps, tail, halo,
    send, recv, local,
):
    at = places()
    s = at["s"]
    peers = ("twin", "up", "down", "across", "right", "left", "pair", "after", "before")
    met = greet(at, peers)
    width, depth = lat.shape[1], wout.shape[0]

    def load(index, source, target):
        copy = pltpu.make_async_copy(source, target, local.at[index])
        copy.start()
        return copy

    first_loads = [load(0, lat_in, lat), load(1, mod_in, mod), load(2, gain_in, gain)]
    weights = [load(3 + j, wqkv.at[j], wbuf.at[j]) for j in range(3)]
    late_loads = [
        load(6, wout, obuf.at[pl.ds(0, depth)]),
        load(7, whead, heads.at[pl.ds(0, 96)]),
        load(8, conv_w, taps.at[:, pl.ds(0, 96)]),
    ]
    for item in first_loads:
        item.wait()
    level = levels[0]
    shift = mod[0, pl.ds(level, 1), :]
    scale = 1.0 + mod[1, pl.ds(level, 1), :]
    for row in range(0, TOK_DEV, 16):
        values = lat[row : row + 16, :].astype(F32)
        centre = values - jnp.mean(values, -1, keepdims=True)
        spread = jnp.mean(centre * centre, -1, keepdims=True)
        xbuf[row : row + 16, :] = (centre * lax.rsqrt(spread + EPS) * scale + shift).astype(BF16)
    met()
    post = Post(send, recv)

    def part(place, core, half):
        return xbuf.at[pl.ds((place * 2 + core) * TOK_DEV + half * HALF, HALF)]

    twin = {}

    def hand(place, half):
        twin[place, half] = post(part(place, 0, half), part(place, 1, half), at["twin"])

    def move(source, target, half, to):
        return post(part(source, 0, half), part(target, 0, half), at[to])

    def settle(*names):
        for place in names:
            for half in range(2):
                twin[place, half].wait_recv()

    up, down, across = {}, {}, {}
    for first in (0, 1):
        up[first] = move(OWN, DOWN, first, "up")
        down[1 - first] = move(OWN, UP, 1 - first, "down")
        across[first] = move(OWN, ACROSS, first, "across")
        hand(OWN, first)
    wtwin = post(wout, obuf.at[pl.ds(depth, depth)], at["twin"])

    def project(group):
        start, rows = GROUPS[group]
        tiles = rows // TOK_DEV
        x = xbuf[start : start + rows, :]
        for j, out in enumerate((qbuf, kbuf, vbuf)):
            p = jnp.dot(x, wbuf[j], preferred_element_type=F32)
            if j < 2:
                parts = []
                for h in range(2):
                    t = p[:, h * HD : (h + 1) * HD]
                    square = jnp.mean(t * t, -1, keepdims=True)
                    g = gain[j : j + 1, h * HD : (h + 1) * HD]
                    if j == 0:
                        g = g * (LOG2E * HD ** (-0.5))
                    parts.append(t * lax.rsqrt(square + EPS) * g)
                p = jnp.concatenate(parts, -1)
            out[start : start + rows, :] = p.astype(BF16)
            if j > 0:
                lead = p.reshape(tiles, FRAMES, SPOTS, WIDE)
                for f in range(KEEP):
                    kvbuf[0, f, start // 8 : (start + rows) // 8, (j - 1) * WIDE : j * WIDE] = (
                        lead[:, f].reshape(tiles * SPOTS, WIDE).astype(BF16)
                    )

    ranges = ((0, 48), (48, 32), (80, 32), (112, 16))

    class Spread:
        def __init__(self, index):
            self.first, self.rows = ranges[index]

        def move(self, source, target, f, to):
            rows = pl.ds(self.first, self.rows)
            return post(kvbuf.at[source, f, rows], kvbuf.at[target, f, rows], at[to])

        def begin(self):
            self.right = [self.move(0, 1, f, "right") for f in range(2)]
            self.left = [self.move(0, 3, f, "left") for f in (1, 0)][::-1]
            self.pair = [self.move(0, 4, f, "pair") for f in range(2)]

        def second(self):
            self.right[0].wait_recv()
            self.far = [self.move(1, 2, 0, "right")]
            self.left[1].wait_recv()
            self.far.append(self.move(3, 2, 1, "left"))
            self.over_right, self.over_left = [], []
            for f in range(2):
                self.pair[f].wait_recv()
                self.over_right.append(self.move(4, 5, f, "right"))
                self.over_left.append(self.move(4, 7, f, "left"))
            self.right[1].wait_recv()
            self.left[0].wait_recv()

        def third(self):
            self.over_right[0].wait_recv()
            self.far.append(self.move(5, 6, 0, "right"))
            self.over_left[1].wait_recv()
            self.far.append(self.move(7, 6, 1, "left"))
            self.over_right[1].wait_recv()
            self.over_left[0].wait_recv()

        def end(self):
            for copy in self.far:
                copy.wait_recv()

    spread = [Spread(index) for index in range(4)]

    settle(OWN)
    for item in weights:
        item.wait()
    project(0)

    far, over, cross_y, over_far = {}, {}, {}, {}
    up[0].wait_recv()
    far[0] = move(DOWN, FAR, 0, "up")
    cross_y[0] = move(DOWN, XDOWN, 0, "across")
    hand(DOWN, 0)
    down[1].wait_recv()
    far[1] = move(UP, FAR, 1, "down")
    cross_y[1] = move(UP, XUP, 1, "across")
    hand(UP, 1)
    across[0].wait_recv()
    over[0] = move(ACROSS, XUP, 0, "down")
    hand(ACROSS, 0)
    up[1].wait_recv()
    hand(DOWN, 1)
    down[0].wait_recv()
    hand(UP, 0)
    across[1].wait_recv()
    over[1] = move(ACROSS, XDOWN, 1, "up")
    hand(ACROSS, 1)
    settle(DOWN, UP)
    project(1)
    spread[0].begin()

    for half in range(2):
        far[half].wait_recv()
        hand(FAR, half)
    cross_y[0].wait_recv()
    over_far[0] = move(XDOWN, XFAR, 0, "up")
    hand(XDOWN, 0)
    settle(FAR, ACROSS)
    project(2)
    spread[1].begin()
    spread[0].second()

    cross_y[1].wait_recv()
    over_far[1] = move(XUP, XFAR, 1, "down")
    hand(XUP, 1)
    over[1].wait_recv()
    hand(XDOWN, 1)
    over[0].wait_recv()
    hand(XUP, 0)
    settle(XDOWN, XUP)
    project(3)
    spread[2].begin()
    spread[0].third()
    spread[1].second()

    for half in range(2):
        over_far[half].wait_recv()
        hand(XFAR, half)
    settle(XFAR)
    project(4)
    spread[3].begin()
    spread[1].third()
    spread[2].second()

    contract = (((1,), (1,)), ((), ()))
    x, yl = s // 2, s % 2
    penalties = []
    for place in range(1, 8):
        source = ((x + 4 - place % 4) % 4) * 2 + (yl + place // 4) % 2
        seen = (source < s) & (visible[s, source] == 1)
        count = counts[source]
        penalties.append(
            [jnp.where(seen & (f < count), 0.0, PENALTY).astype(F32) for f in range(KEEP)]
        )

    def queries(place):
        return pl.ds(place * 128, 128)

    def own_clip(place):
        rows = queries(place)
        for h in range(2):
            cols = slice(h * HD, (h + 1) * HD)
            scores = lax.dot_general(
                qbuf[rows, cols], kbuf[:, cols], contract, preferred_element_type=F32
            )
            top = jnp.max(scores, -1, keepdims=True)
            terms = jnp.exp2(scores - top)
            best[h, rows] = top
            total[h, rows] = jnp.sum(terms, -1, keepdims=True)
            acc[h, rows] = jnp.dot(
                terms.astype(BF16), vbuf[:, cols], preferred_element_type=F32
            )

    def earlier_clips(place):
        rows = queries(place)
        for h in range(2):
            cols = slice(h * HD, (h + 1) * HD)
            query = qbuf[rows, cols]
            old = best[h, rows]
            top = old
            scores = []
            for i in range(7):
                for f in range(KEEP):
                    piece = lax.dot_general(
                        query, kvbuf[i + 1, f, :, cols], contract, preferred_element_type=F32
                    )
                    scores.append(piece)
                    top = jnp.maximum(
                        top, jnp.max(piece, -1, keepdims=True) - penalties[i][f]
                    )
            decay = jnp.exp2(old - top)
            terms = [
                jnp.exp2(piece - (top + penalties[n // 2][n % 2]))
                for n, piece in enumerate(scores)
            ]
            plain = terms[0]
            for term in terms[1:]:
                plain = plain + term
            norm = total[h, rows] * decay + jnp.sum(plain, -1, keepdims=True)
            values = kvbuf[1:8, :, :, WIDE + h * HD : WIDE + (h + 1) * HD].reshape(7 * WIDE, HD)
            mixed = acc[h, rows] * decay + jnp.dot(
                jnp.concatenate([term.astype(BF16) for term in terms], -1),
                values,
                preferred_element_type=F32,
            )
            out = (mixed / norm).astype(BF16)
            att[place, 0, :, cols] = out[:TOK_DEV]
            att[place, 1, :, cols] = out[TOK_DEV:]

    shared = {}

    def swap(place):
        shared[place] = post(att.at[place, 1], atwin.at[place], at["twin"])

    tile = 512

    def multiply(*spots):
        for p in spots:
            shared[p].wait_recv()
        a = jnp.concatenate(
            [jnp.concatenate([att[p, 0], atwin[p]], -1) for p in spots], 0
        )
        for col in range(0, width, tile):
            r = jnp.dot(a, obuf[:, col : col + tile], preferred_element_type=F32)
            for i, p in enumerate(spots):
                partial[p, :, col : col + tile] = r[i * TOK_DEV : (i + 1) * TOK_DEV]

    def ship(spot, half, box, to, *added):
        rows = slice(half * HALF, (half + 1) * HALF)
        value = partial[spot, rows, :]
        for other in added:
            value = value + other[rows, :].astype(F32)
        outbox[spot, rows, :] = value.astype(BF16)
        piece = pl.ds(half * HALF, HALF)
        return post(outbox.at[spot, piece], box.at[piece], at[to])

    own_clip(XFAR)
    spread[2].third()
    spread[3].second()
    own_clip(XDOWN)
    spread[3].third()
    own_clip(XUP)
    for item in spread:
        item.end()
    earlier_clips(XFAR)
    swap(XFAR)
    for item in late_loads:
        item.wait()
    wtwin.wait_recv()
    heads[96:, :] = jnp.zeros((32, width), BF16)
    taps[:, 96:, :] = jnp.zeros((3, 32, taps.shape[2]), BF16)
    multiply(XFAR)
    fx0 = ship(XFAR, 0, fx, "up")
    fx1 = ship(XFAR, 1, fx, "down")

    earlier_clips(XDOWN)
    swap(XDOWN)
    earlier_clips(XUP)
    swap(XUP)
    own_clip(FAR)
    multiply(XDOWN, XUP)
    cx1 = ship(XUP, 1, cx, "up")
    cx0 = ship(XDOWN, 0, cx, "down")
    earlier_clips(FAR)
    swap(FAR)
    fx0.wait_recv()
    yx0 = ship(XUP, 0, yx, "across", fx)
    fx1.wait_recv()
    yx1 = ship(XDOWN, 1, yx, "across", fx)
    multiply(FAR)
    fo0 = ship(FAR, 0, fo, "up")
    fo1 = ship(FAR, 1, fo, "down")

    def rest(index, carry):
        own_clip(index)
        earlier_clips(index)
        return carry

    lax.fori_loop(DOWN, UP + 1, rest, 0)
    swap(DOWN)
    swap(UP)
    own_clip(ACROSS)
    multiply(DOWN, UP)
    zd1 = ship(UP, 1, zd, "up")
    zu0 = ship(DOWN, 0, zu, "down")
    earlier_clips(ACROSS)
    swap(ACROSS)
    own_clip(OWN)
    multiply(ACROSS)
    cx1.wait_recv()
    ya1 = ship(ACROSS, 1, ya, "across", cx)
    cx0.wait_recv()
    ya0 = ship(ACROSS, 0, ya, "across", cx)
    fo0.wait_recv()
    yx0.wait_recv()
    zd0 = ship(UP, 0, zd, "up", fo, yx)
    fo1.wait_recv()
    yx1.wait_recv()
    zu1 = ship(DOWN, 1, zu, "down", fo, yx)
    earlier_clips(OWN)
    swap(OWN)
    multiply(OWN)

    gate = mod[2, pl.ds(level, 1), :]
    for copy in (zd1, zu0, ya1, zd0, zu1, ya0):
        copy.wait_recv()
    for row in range(0, TOK_DEV, 16):
        piece = slice(row, row + 16)
        mixed = partial[OWN, piece, :]
        for box in (zd, zu, ya):
            mixed = mixed + box[piece, :].astype(F32)
        den[piece, :] = (lat[piece, :].astype(F32) + gate * mixed).astype(BF16)
    feats = lax.dot_general(
        den[...], heads[...], contract, preferred_element_type=F32
    ).astype(BF16).astype(F32)
    tail[...] = feats[TOK_DEV - 2 * SPOTS :].astype(BF16)
    edge = post(tail, halo, at["after"])
    edge.wait_recv()
    earlier = jnp.where(s > 0, halo[...].astype(F32), 0.0)
    sequence = jnp.concatenate([earlier, feats], 0)
    conv = jnp.zeros(dec.shape, F32)
    for tap in range(3):
        begin = (2 - tap) * SPOTS
        window = sequence[begin : begin + TOK_DEV].astype(BF16)
        conv = conv + jnp.dot(window, taps[tap], preferred_element_type=F32)
    dec[...] = (conv / (1.0 + jnp.exp(-conv))).astype(BF16)
    post.drain()
    assert len(post.copies) == COPIES


def layer(levels, visible, counts, lat, mod, wqkv, gain, wout, whead, conv_w):
    rows, width, depth = 16 * TOK_DEV, lat.shape[1], wout.shape[0]
    vmem = pl.BlockSpec(memory_space=pltpu.VMEM)
    smem = pl.BlockSpec(memory_space=pltpu.SMEM)
    hbm = pl.BlockSpec(memory_space=pltpu.HBM)
    block = pltpu.VMEM((TOK_DEV, width), BF16)
    edge = pltpu.VMEM((2 * SPOTS, 128), BF16)
    return pl.pallas_call(
        layer_kernel,
        out_shape=(
            jax.ShapeDtypeStruct(lat.shape, BF16),
            jax.ShapeDtypeStruct((lat.shape[0], conv_w.shape[2]), BF16),
        ),
        in_specs=[smem, smem, smem] + [hbm] * 7,
        out_specs=(vmem, vmem),
        scratch_shapes=[
            block,
            pltpu.VMEM(mod.shape, F32),
            pltpu.VMEM(gain.shape, F32),
            pltpu.VMEM((rows, width), BF16),
            pltpu.VMEM((3, width, WIDE), BF16),
            pltpu.VMEM((rows, WIDE), BF16),
            pltpu.VMEM((rows, WIDE), BF16),
            pltpu.VMEM((rows, WIDE), BF16),
            pltpu.VMEM((8, KEEP, 128, 2 * WIDE), BF16),
            pltpu.VMEM((2, rows, 1), F32),
            pltpu.VMEM((2, rows, 1), F32),
            pltpu.VMEM((2, rows, HD), F32),
            pltpu.VMEM((8, 2, TOK_DEV, WIDE), BF16),
            pltpu.VMEM((8, TOK_DEV, WIDE), BF16),
            pltpu.VMEM((2 * depth, width), BF16),
            pltpu.VMEM((8, TOK_DEV, width), F32),
            pltpu.VMEM((8, TOK_DEV, width), BF16),
            block, block, block, block, block, block, block,
            pltpu.VMEM((128, width), BF16),
            pltpu.VMEM((3, 128, conv_w.shape[2]), BF16),
            edge,
            edge,
            pltpu.SemaphoreType.DMA((COPIES,)),
            pltpu.SemaphoreType.DMA((COPIES,)),
            pltpu.SemaphoreType.DMA((9,)),
        ],
        compiler_params=pltpu.CompilerParams(
            collective_id=0, has_side_effects=True, vmem_limit_bytes=58 * 2**20
        ),
        name="layer",
    )(levels, visible, counts, lat, mod, wqkv, gain, wout, whead, conv_w)


def per_device(
    latents, levels, visible, frame_counts, modulation, w_qkv, qk_gain, w_out, w_head, conv_w
):
    denoised, decoded = layer(
        levels, visible, frame_counts, latents[0], modulation.transpose(1, 0, 2),
        w_qkv.transpose(1, 0, 2), qk_gain, w_out, w_head.T, conv_w,
    )
    return (denoised[None], decoded[None])


def solution(mesh):
    placed = (
        P("span", "tok", None),
        P("span"),
        P(),
        P(),
        P(),
        P(None, None, "tok"),
        P(None, "tok"),
        P("tok", None),
        P(),
        P(),
    )
    return jax.shard_map(
        per_device,
        mesh=mesh,
        in_specs=placed,
        out_specs=(P("span", "tok", None), P("span", "tok", None)),
        check_vma=False,
    )
```

time: 123 us -> 100 us (0.81)
  Pallas kernels: 115 us -> 95.5 us
  local copies, waits for them, and re-layouts: 5.71 us -> 3.24 us
    pallas_call x3 -> x1, Pallas kernels: 115 us -> 95.5 us  [layer(): pl.pallas_call(layer_kernel, out_shape=(jax.ShapeDtypeStruct(lat.shape, B...]
    unnamed x20 -> x2, local copies, waits for them, and re-layouts: 5.71 us -> 3.24 us
where the time goes in v2:
time: 100 us
  Pallas kernels  95.5 us (96%)
  local copies, waits for them, and re-layouts  3.24 us (3%)
  between operations  1.29 us (1%)
    pallas_call x1, Pallas kernels, layer(): pl.pallas_call(layer_kernel, out_shape=(jax.ShapeDtypeStruct(lat.shape, B...  95.5 us
    unnamed x2, local copies, waits for them, and re-layouts  3.24 us

profile of v2, /device:TPU:0, one launch (start us, length us, event | category | flops | bytes accessed | tf_op | source)
XLA Modules:
  0.0 100.1 jit_solution(879231396028715293)
XLA Ops:
  1.3 95.5 %layer.1 = (bf16[64,3584]{1,0:T(8,128)(2,1)}, bf16[64,384]{1,0:T(8,128)(2,1)}) custom-call(s32[1]{0:T(128)S(6)} %copy.14.levels, s32[8,8]{1,0:T(8,128)} %visible.1, s32[8]{0:T(128)} %counts.1, bf16[64,3584]{1,0:T(8,128)(2,1)} %bitcast.10, f32[3,16,3584]{2,1,0:T(8,128)} %bitcast.7, bf16[3,3584,256]{2,1,0:T(8,128)(2,1)} %bitcast.6, f32[2,256]{1,0:T(2,128)} %gain_in.1, ...), custom_call_target="tpu_custom_call" | custom-call | tf_op jit(solution)/shard_map/layer/pallas_call | solution.py:464
  96.8 1.8 %copy.15 = bf16[1,64,3584]{2,1,0:T(8,128)(2,1)} copy(bf16[1,64,3584]{2,1,0:T(8,128)(2,1)} %bitcast.9) | data formatting | bytes 917504
  98.6 1.4 %copy.16 = bf16[1,64,384]{2,1,0:T(8,128)(2,1)} copy(bf16[1,64,384]{2,1,0:T(8,128)(2,1)} %bitcast.11) | data formatting | bytes 98304

commit v3 on v2

--- a/solution.py
+++ b/solution.py
@@ -73,17 +73,18 @@
         for copy in self.copies:
             copy.wait_send()
 
-COPIES = 30 + 56 + 1 + 8 + 14 + 1
-GROUPS = ((0, 128), (128, 256), (384, 256), (640, 256), (896, 128))
+COPIES = 60 + 14 + 1 + 8 + 14 + 1
+LEAD = KEEP * SPOTS
+REST = TOK_DEV - LEAD
 PENALTY = 1e30
 WIDE = 2 * HD
 
 
 def layer_kernel(
-    levels, visible, counts, lat_in, mod_in, wqkv, gain_in, wout, whead, conv_w,
-    den, dec,
-    lat, mod, gain, xbuf, wbuf, qbuf, kbuf, vbuf, kvbuf, best, total, acc, att, atwin,
-    obuf, partial, outbox, fx, cx, fo, yx, zd, zu, ya, heads, taps, tail, halo,
+    levels, visible, counts, lat_in, mod_in, wqkv, gain_in, wout, whead,
+    den, seq,
+    lat, mod, gain, xlead, xrest, wbuf, qbuf, kbuf, vbuf, kvbuf, best, total, acc, att, atwin,
+    obuf, partial, outbox, fx, cx, fo, yx, zd, zu, ya, heads, tail, halo,
     send, recv, local,
 ):
     at = places()
@@ -102,49 +103,108 @@
     late_loads = [
         load(6, wout, obuf.at[pl.ds(0, depth)]),
         load(7, whead, heads.at[pl.ds(0, 96)]),
-        load(8, conv_w, taps.at[:, pl.ds(0, 96)]),
     ]
     for item in first_loads:
         item.wait()
     level = levels[0]
     shift = mod[0, pl.ds(level, 1), :]
     scale = 1.0 + mod[1, pl.ds(level, 1), :]
-    for row in range(0, TOK_DEV, 16):
-        values = lat[row : row + 16, :].astype(F32)
+
+    def modulate(row, target, place):
+        values = lat[row : row + LEAD, :].astype(F32)
         centre = values - jnp.mean(values, -1, keepdims=True)
         spread = jnp.mean(centre * centre, -1, keepdims=True)
-        xbuf[row : row + 16, :] = (centre * lax.rsqrt(spread + EPS) * scale + shift).astype(BF16)
+        target[place : place + LEAD, :] = (
+            centre * lax.rsqrt(spread + EPS) * scale + shift
+        ).astype(BF16)
+
+    modulate(0, xlead, 0)
     met()
     post = Post(send, recv)
 
-    def part(place, core, half):
-        return xbuf.at[pl.ds((place * 2 + core) * TOK_DEV + half * HALF, HALF)]
-
-    twin = {}
-
-    def hand(place, half):
-        twin[place, half] = post(part(place, 0, half), part(place, 1, half), at["twin"])
-
-    def move(source, target, half, to):
-        return post(part(source, 0, half), part(target, 0, half), at[to])
-
-    def settle(*names):
-        for place in names:
+    class Gather:
+        def __init__(self, buffer, rows):
+            self.buffer, self.rows = buffer, rows
+            self.twin, self.up, self.down, self.across = {}, {}, {}, {}
+            self.far, self.over, self.cross_y, self.over_far = {}, {}, {}, {}
+
+        def part(self, place, core, half):
+            return self.buffer.at[
+                pl.ds((place * 2 + core) * self.rows, self.rows),
+                pl.ds(half * (width // 2), width // 2),
+            ]
+
+        def hand(self, place, half):
+            self.twin[place, half] = post(
+                self.part(place, 0, half), self.part(place, 1, half), at["twin"]
+            )
+
+        def move(self, source, target, half, to):
+            return post(self.part(source, 0, half), self.part(target, 0, half), at[to])
+
+        def settle(self, *names):
+            for place in names:
+                for half in range(2):
+                    self.twin[place, half].wait_recv()
+
+        def begin(self):
+            for first in (0, 1):
+                self.up[first] = self.move(OWN, DOWN, first, "up")
+                self.down[1 - first] = self.move(OWN, UP, 1 - first, "down")
+                self.across[first] = self.move(OWN, ACROSS, first, "across")
+                self.hand(OWN, first)
+
+        def near(self):
+            self.up[0].wait_recv()
+            self.far[0] = self.move(DOWN, FAR, 0, "up")
+            self.cross_y[0] = self.move(DOWN, XDOWN, 0, "across")
+            self.hand(DOWN, 0)
+            self.down[1].wait_recv()
+            self.far[1] = self.move(UP, FAR, 1, "down")
+            self.cross_y[1] = self.move(UP, XUP, 1, "across")
+            self.hand(UP, 1)
+            self.across[0].wait_recv()
+            self.over[0] = self.move(ACROSS, XUP, 0, "down")
+            self.hand(ACROSS, 0)
+            self.across[1].wait_recv()
+            self.over[1] = self.move(ACROSS, XDOWN, 1, "up")
+            self.hand(ACROSS, 1)
+            self.up[1].wait_recv()
+            self.hand(DOWN, 1)
+            self.down[0].wait_recv()
+            self.hand(UP, 0)
+
+        def turn(self, half):
+            self.cross_y[half].wait_recv()
+            source, to = ((XDOWN, "up"), (XUP, "down"))[half]
+            self.over_far[half] = self.move(source, XFAR, half, to)
+            self.hand(source, half)
+
+        def opposite(self):
             for half in range(2):
-                twin[place, half].wait_recv()
-
-    up, down, across = {}, {}, {}
-    for first in (0, 1):
-        up[first] = move(OWN, DOWN, first, "up")
-        down[1 - first] = move(OWN, UP, 1 - first, "down")
-        across[first] = move(OWN, ACROSS, first, "across")
-        hand(OWN, first)
-    wtwin = post(wout, obuf.at[pl.ds(depth, depth)], at["twin"])
-
-    def project(group):
-        start, rows = GROUPS[group]
-        tiles = rows // TOK_DEV
-        x = xbuf[start : start + rows, :]
+                self.far[half].wait_recv()
+                self.hand(FAR, half)
+
+        def beside(self):
+            self.over[1].wait_recv()
+            self.hand(XDOWN, 1)
+            self.over[0].wait_recv()
+            self.hand(XUP, 0)
+
+        def last(self):
+            for half in range(2):
+                self.over_far[half].wait_recv()
+                self.hand(XFAR, half)
+
+    early = Gather(xlead, LEAD)
+    later = Gather(xrest, REST)
+    early.begin()
+    for row in range(LEAD, TOK_DEV, LEAD):
+        modulate(row, xrest, row - LEAD)
+
+    def project(slot, tiles, lead):
+        rows = LEAD if lead else REST
+        x = (xlead if lead else xrest)[slot * rows : (slot + tiles) * rows, :]
         for j, out in enumerate((qbuf, kbuf, vbuf)):
             p = jnp.dot(x, wbuf[j], preferred_element_type=F32)
             if j < 2:
@@ -157,116 +217,68 @@
                         g = g * (LOG2E * HD ** (-0.5))
                     parts.append(t * lax.rsqrt(square + EPS) * g)
                 p = jnp.concatenate(parts, -1)
-            out[start : start + rows, :] = p.astype(BF16)
-            if j > 0:
-                lead = p.reshape(tiles, FRAMES, SPOTS, WIDE)
+            first = 0 if lead else LEAD
+            out[slot : slot + tiles, first : first + rows, :] = p.reshape(
+                tiles, rows, WIDE
+            ).astype(BF16)
+            if j > 0 and lead:
+                frames = p.reshape(tiles, KEEP, SPOTS, WIDE)
                 for f in range(KEEP):
-                    kvbuf[0, f, start // 8 : (start + rows) // 8, (j - 1) * WIDE : j * WIDE] = (
-                        lead[:, f].reshape(tiles * SPOTS, WIDE).astype(BF16)
+                    kvbuf[0, f, :, (j - 1) * WIDE : j * WIDE] = (
+                        frames[:, f].reshape(tiles * SPOTS, WIDE).astype(BF16)
                     )
 
-    ranges = ((0, 48), (48, 32), (80, 32), (112, 16))
-
-    class Spread:
-        def __init__(self, index):
-            self.first, self.rows = ranges[index]
-
-        def move(self, source, target, f, to):
-            rows = pl.ds(self.first, self.rows)
-            return post(kvbuf.at[source, f, rows], kvbuf.at[target, f, rows], at[to])
-
-        def begin(self):
-            self.right = [self.move(0, 1, f, "right") for f in range(2)]
-            self.left = [self.move(0, 3, f, "left") for f in (1, 0)][::-1]
-            self.pair = [self.move(0, 4, f, "pair") for f in range(2)]
-
-        def second(self):
-            self.right[0].wait_recv()
-            self.far = [self.move(1, 2, 0, "right")]
-            self.left[1].wait_recv()
-            self.far.append(self.move(3, 2, 1, "left"))
-            self.over_right, self.over_left = [], []
-            for f in range(2):
-                self.pair[f].wait_recv()
-                self.over_right.append(self.move(4, 5, f, "right"))
-                self.over_left.append(self.move(4, 7, f, "left"))
-            self.right[1].wait_recv()
-            self.left[0].wait_recv()
-
-        def third(self):
-            self.over_right[0].wait_recv()
-            self.far.append(self.move(5, 6, 0, "right"))
-            self.over_left[1].wait_recv()
-            self.far.append(self.move(7, 6, 1, "left"))
-            self.over_right[1].wait_recv()
-            self.over_left[0].wait_recv()
-
-        def end(self):
-            for copy in self.far:
-                copy.wait_recv()
-
-    spread = [Spread(index) for index in range(4)]
-
-    settle(OWN)
+    def spread(source, target, f, to):
+        return post(kvbuf.at[source, f], kvbuf.at[target, f], at[to])
+
+    early.near()
+    early.turn(0)
+    early.turn(1)
+    later.begin()
+    wtwin = post(wout, obuf.at[pl.ds(depth, depth)], at["twin"])
+    early.opposite()
+    early.beside()
+    early.last()
     for item in weights:
         item.wait()
-    project(0)
-
-    far, over, cross_y, over_far = {}, {}, {}, {}
-    up[0].wait_recv()
-    far[0] = move(DOWN, FAR, 0, "up")
-    cross_y[0] = move(DOWN, XDOWN, 0, "across")
-    hand(DOWN, 0)
-    down[1].wait_recv()
-    far[1] = move(UP, FAR, 1, "down")
-    cross_y[1] = move(UP, XUP, 1, "across")
-    hand(UP, 1)
-    across[0].wait_recv()
-    over[0] = move(ACROSS, XUP, 0, "down")
-    hand(ACROSS, 0)
-    up[1].wait_recv()
-    hand(DOWN, 1)
-    down[0].wait_recv()
-    hand(UP, 0)
-    across[1].wait_recv()
-    over[1] = move(ACROSS, XDOWN, 1, "up")
-    hand(ACROSS, 1)
-    settle(DOWN, UP)
-    project(1)
-    spread[0].begin()
-
-    for half in range(2):
-        far[half].wait_recv()
-        hand(FAR, half)
-    cross_y[0].wait_recv()
-    over_far[0] = move(XDOWN, XFAR, 0, "up")
-    hand(XDOWN, 0)
-    settle(FAR, ACROSS)
-    project(2)
-    spread[1].begin()
-    spread[0].second()
-
-    cross_y[1].wait_recv()
-    over_far[1] = move(XUP, XFAR, 1, "down")
-    hand(XUP, 1)
-    over[1].wait_recv()
-    hand(XDOWN, 1)
-    over[0].wait_recv()
-    hand(XUP, 0)
-    settle(XDOWN, XUP)
-    project(3)
-    spread[2].begin()
-    spread[0].third()
-    spread[1].second()
-
-    for half in range(2):
-        over_far[half].wait_recv()
-        hand(XFAR, half)
-    settle(XFAR)
-    project(4)
-    spread[3].begin()
-    spread[1].third()
-    spread[2].second()
+    early.settle(*range(8))
+    project(0, 16, True)
+    right = [spread(0, 1, f, "right") for f in (0, 1)]
+    left = [spread(0, 3, f, "left") for f in (1, 0)][::-1]
+    later.near()
+    pair = [spread(0, 4, f, "pair") for f in (0, 1)]
+    later.settle(OWN)
+    project(0, 2, False)
+    later.settle(DOWN, UP)
+    right[0].wait_recv()
+    far = [spread(1, 2, 0, "right")]
+    left[1].wait_recv()
+    far.append(spread(3, 2, 1, "left"))
+    project(2, 4, False)
+    later.turn(0)
+    later.opposite()
+    later.settle(FAR, ACROSS)
+    later.turn(1)
+    project(6, 4, False)
+    later.beside()
+    over_right, over_left = {}, {}
+
+    def cross(f):
+        pair[f].wait_recv()
+        over_right[f] = spread(4, 5, f, "right")
+        over_left[f] = spread(4, 7, f, "left")
+
+    cross(0)
+    later.settle(XDOWN, XUP)
+    project(10, 4, False)
+    cross(1)
+    later.last()
+    over_right[0].wait_recv()
+    far.append(spread(5, 6, 0, "right"))
+    later.settle(XFAR)
+    project(14, 2, False)
+    over_left[1].wait_recv()
+    far.append(spread(7, 6, 1, "left"))
 
     contract = (((1,), (1,)), ((), ()))
     x, yl = s // 2, s % 2
@@ -282,26 +294,31 @@
     def queries(place):
         return pl.ds(place * 128, 128)
 
+    def tiles_of(place, cols):
+        return qbuf[pl.ds(2 * place, 2), :, cols].reshape(128, HD)
+
     def own_clip(place):
         rows = queries(place)
         for h in range(2):
             cols = slice(h * HD, (h + 1) * HD)
             scores = lax.dot_general(
-                qbuf[rows, cols], kbuf[:, cols], contract, preferred_element_type=F32
+                tiles_of(place, cols), kbuf[:, :, cols].reshape(16 * TOK_DEV, HD), contract,
+                preferred_element_type=F32,
             )
             top = jnp.max(scores, -1, keepdims=True)
             terms = jnp.exp2(scores - top)
             best[h, rows] = top
             total[h, rows] = jnp.sum(terms, -1, keepdims=True)
             acc[h, rows] = jnp.dot(
-                terms.astype(BF16), vbuf[:, cols], preferred_element_type=F32
+                terms.astype(BF16), vbuf[:, :, cols].reshape(16 * TOK_DEV, HD),
+                preferred_element_type=F32,
             )
 
     def earlier_clips(place):
         rows = queries(place)
         for h in range(2):
             cols = slice(h * HD, (h + 1) * HD)
-            query = qbuf[rows, cols]
+            query = tiles_of(place, cols)
             old = best[h, rows]
             top = old
             scores = []
@@ -361,20 +378,16 @@
         return post(outbox.at[spot, piece], box.at[piece], at[to])
 
     own_clip(XFAR)
-    spread[2].third()
-    spread[3].second()
     own_clip(XDOWN)
-    spread[3].third()
     own_clip(XUP)
-    for item in spread:
-        item.end()
+    for copy in (right[1], left[0], over_right[1], over_left[0], *far):
+        copy.wait_recv()
     earlier_clips(XFAR)
     swap(XFAR)
     for item in late_loads:
         item.wait()
     wtwin.wait_recv()
     heads[96:, :] = jnp.zeros((32, width), BF16)
-    taps[:, 96:, :] = jnp.zeros((3, 32, taps.shape[2]), BF16)
     multiply(XFAR)
     fx0 = ship(XFAR, 0, fx, "up")
     fx1 = ship(XFAR, 1, fx, "down")
@@ -443,18 +456,42 @@
     edge = post(tail, halo, at["after"])
     edge.wait_recv()
     earlier = jnp.where(s > 0, halo[...].astype(F32), 0.0)
-    sequence = jnp.concatenate([earlier, feats], 0)
+    seq[: 2 * SPOTS, :] = earlier.astype(BF16)
+    seq[2 * SPOTS :, :] = feats.astype(BF16)
+    post.drain()
+    assert len(post.copies) == COPIES
+
+
+def decode_kernel(den_in, seq, conv_w, den, dec, taps):
+    den[...] = den_in[...]
+    taps[:, 96:, :] = jnp.zeros((3, 32, taps.shape[2]), BF16)
+    taps[:, :96, :] = conv_w[...]
+    sequence = seq[...].astype(F32)
     conv = jnp.zeros(dec.shape, F32)
     for tap in range(3):
         begin = (2 - tap) * SPOTS
         window = sequence[begin : begin + TOK_DEV].astype(BF16)
         conv = conv + jnp.dot(window, taps[tap], preferred_element_type=F32)
     dec[...] = (conv / (1.0 + jnp.exp(-conv))).astype(BF16)
-    post.drain()
-    assert len(post.copies) == COPIES
-
-
-def layer(levels, visible, counts, lat, mod, wqkv, gain, wout, whead, conv_w):
+
+
+def decode(den, seq, conv_w):
+    vmem = pl.BlockSpec(memory_space=pltpu.VMEM)
+    return pl.pallas_call(
+        decode_kernel,
+        out_shape=(
+            jax.ShapeDtypeStruct(den.shape, BF16),
+            jax.ShapeDtypeStruct((den.shape[0], conv_w.shape[2]), BF16),
+        ),
+        in_specs=[vmem] * 3,
+        out_specs=(vmem, vmem),
+        scratch_shapes=[pltpu.VMEM((3, 128, conv_w.shape[2]), BF16)],
+        compiler_params=pltpu.CompilerParams(vmem_limit_bytes=58 * 2**20),
+        name="decode",
+    )(den, seq, conv_w)
+
+
+def layer(levels, visible, counts, lat, mod, wqkv, gain, wout, whead):
     rows, width, depth = 16 * TOK_DEV, lat.shape[1], wout.shape[0]
     vmem = pl.BlockSpec(memory_space=pltpu.VMEM)
     smem = pl.BlockSpec(memory_space=pltpu.SMEM)
@@ -465,19 +502,20 @@
         layer_kernel,
         out_shape=(
             jax.ShapeDtypeStruct(lat.shape, BF16),
-            jax.ShapeDtypeStruct((lat.shape[0], conv_w.shape[2]), BF16),
+            jax.ShapeDtypeStruct((lat.shape[0] + 2 * SPOTS, 128), BF16),
         ),
-        in_specs=[smem, smem, smem] + [hbm] * 7,
+        in_specs=[smem, smem, smem] + [hbm] * 6,
         out_specs=(vmem, vmem),
         scratch_shapes=[
             block,
             pltpu.VMEM(mod.shape, F32),
             pltpu.VMEM(gain.shape, F32),
-            pltpu.VMEM((rows, width), BF16),
+            pltpu.VMEM((16 * LEAD, width), BF16),
+            pltpu.VMEM((16 * REST, width), BF16),
             pltpu.VMEM((3, width, WIDE), BF16),
-            pltpu.VMEM((rows, WIDE), BF16),
-            pltpu.VMEM((rows, WIDE), BF16),
-            pltpu.VMEM((rows, WIDE), BF16),
+            pltpu.VMEM((16, TOK_DEV, WIDE), BF16),
+            pltpu.VMEM((16, TOK_DEV, WIDE), BF16),
+            pltpu.VMEM((16, TOK_DEV, WIDE), BF16),
             pltpu.VMEM((8, KEEP, 128, 2 * WIDE), BF16),
             pltpu.VMEM((2, rows, 1), F32),
             pltpu.VMEM((2, rows, 1), F32),
@@ -489,27 +527,27 @@
             pltpu.VMEM((8, TOK_DEV, width), BF16),
             block, block, block, block, block, block, block,
             pltpu.VMEM((128, width), BF16),
-            pltpu.VMEM((3, 128, conv_w.shape[2]), BF16),
             edge,
             edge,
             pltpu.SemaphoreType.DMA((COPIES,)),
             pltpu.SemaphoreType.DMA((COPIES,)),
-            pltpu.SemaphoreType.DMA((9,)),
+            pltpu.SemaphoreType.DMA((8,)),
         ],
         compiler_params=pltpu.CompilerParams(
             collective_id=0, has_side_effects=True, vmem_limit_bytes=58 * 2**20
         ),
         name="layer",
-    )(levels, visible, counts, lat, mod, wqkv, gain, wout, whead, conv_w)
+    )(levels, visible, counts, lat, mod, wqkv, gain, wout, whead)
 
 
 def per_device(
     latents, levels, visible, frame_counts, modulation, w_qkv, qk_gain, w_out, w_head, conv_w
 ):
-    denoised, decoded = layer(
+    denoised, sequence = layer(
         levels, visible, frame_counts, latents[0], modulation.transpose(1, 0, 2),
-        w_qkv.transpose(1, 0, 2), qk_gain, w_out, w_head.T, conv_w,
+        w_qkv.transpose(1, 0, 2), qk_gain, w_out, w_head.T,
     )
+    denoised, decoded = decode(denoised, sequence, conv_w)
     return (denoised[None], decoded[None])
 
 

time: 100 us -> 93.4 us (0.934)
  Pallas kernels: 95.5 us -> 92 us
  local copies, waits for them, and re-layouts: 3.24 us -> 0 us
    pallas_call x1, Pallas kernels: 95.5 us -> 90 us  [layer(): pl.pallas_call(layer_kernel, out_shape=(jax.ShapeDtypeStruct(lat.shape, B...]
    unnamed x2 -> x0, local copies, waits for them, and re-layouts: 3.24 us -> none
    pallas_call x0 -> x1, Pallas kernels: none -> 1.95 us  [decode(): pl.pallas_call(decode_kernel, out_shape=(jax.ShapeDtypeStruct(den.shape,...]
where the time goes in v3:
time: 93.4 us; the launch traced here: 93.3 us
  Pallas kernels  92 us (99%)
  between operations  1.29 us (1%)
    pallas_call x1, Pallas kernels, layer(): pl.pallas_call(layer_kernel, out_shape=(jax.ShapeDtypeStruct(lat.shape, B...  90 us
    pallas_call x1, Pallas kernels, decode(): pl.pallas_call(decode_kernel, out_shape=(jax.ShapeDtypeStruct(den.shape,...  1.95 us

profile of v3, /device:TPU:0, one launch (start us, length us, event | category | flops | bytes accessed | tf_op | source)
XLA Modules:
  0.0 93.3 jit_solution(8904785045367624047)
XLA Ops:
  1.3 90.0 %layer.1 = (bf16[64,3584]{1,0:T(8,128)(2,1)}, bf16[80,128]{1,0:T(8,128)(2,1)}) custom-call(s32[1]{0:T(128)S(6)} %copy.12.levels, s32[8,8]{1,0:T(8,128)} %visible.1, s32[8]{0:T(128)} %counts.1, bf16[64,3584]{1,0:T(8,128)(2,1)} %bitcast.9, f32[3,16,3584]{2,1,0:T(8,128)} %bitcast.7, bf16[3,3584,256]{2,1,0:T(8,128)(2,1)} %bitcast.6, f32[2,256]{1,0:T(2,128)} %gain_in.1, ...), custom_call_target="tpu_custom_call" | custom-call | tf_op jit(solution)/shard_map/layer/pallas_call | solution.py:501
  91.3 1.9 %decode.1 = (bf16[64,3584]{1,0:T(8,128)(2,1)}, bf16[64,384]{1,0:T(8,128)(2,1)}) custom-call(bf16[64,3584]{1,0:T(8,128)(2,1)} %get-tuple-element.6.den_in, bf16[80,128]{1,0:T(8,128)(2,1)} %get-tuple-element.7.seq, bf16[3,96,384]{2,1,0:T(8,128)(2,1)} %conv_w.1), custom_call_target="tpu_custom_call" | custom-call | tf_op jit(solution)/shard_map/decode/pallas_call | solution.py:480

commit v4 on v3

--- a/solution.py
+++ b/solution.py
@@ -291,18 +291,18 @@
             [jnp.where(seen & (f < count), 0.0, PENALTY).astype(F32) for f in range(KEEP)]
         )
 
-    def queries(place):
-        return pl.ds(place * 128, 128)
-
-    def tiles_of(place, cols):
-        return qbuf[pl.ds(2 * place, 2), :, cols].reshape(128, HD)
-
-    def own_clip(place):
-        rows = queries(place)
+    def queries(place, count):
+        return pl.ds(place * 128, count * 128)
+
+    def tiles_of(place, count, cols):
+        return qbuf[pl.ds(2 * place, 2 * count), :, cols].reshape(128 * count, HD)
+
+    def own_clip(place, count=1):
+        rows = queries(place, count)
         for h in range(2):
             cols = slice(h * HD, (h + 1) * HD)
             scores = lax.dot_general(
-                tiles_of(place, cols), kbuf[:, :, cols].reshape(16 * TOK_DEV, HD), contract,
+                tiles_of(place, count, cols), kbuf[:, :, cols].reshape(16 * TOK_DEV, HD), contract,
                 preferred_element_type=F32,
             )
             top = jnp.max(scores, -1, keepdims=True)
@@ -314,28 +314,25 @@
                 preferred_element_type=F32,
             )
 
-    def earlier_clips(place):
-        rows = queries(place)
+    def earlier_clips(place, count=1):
+        rows = queries(place, count)
         for h in range(2):
             cols = slice(h * HD, (h + 1) * HD)
-            query = tiles_of(place, cols)
+            query = tiles_of(place, count, cols)
             old = best[h, rows]
-            top = old
             scores = []
             for i in range(7):
                 for f in range(KEEP):
                     piece = lax.dot_general(
                         query, kvbuf[i + 1, f, :, cols], contract, preferred_element_type=F32
                     )
-                    scores.append(piece)
-                    top = jnp.maximum(
-                        top, jnp.max(piece, -1, keepdims=True) - penalties[i][f]
-                    )
+                    scores.append(piece - penalties[i][f])
+            peak = scores[0]
+            for score in scores[1:]:
+                peak = jnp.maximum(peak, score)
+            top = jnp.maximum(old, jnp.max(peak, -1, keepdims=True))
             decay = jnp.exp2(old - top)
-            terms = [
-                jnp.exp2(piece - (top + penalties[n // 2][n % 2]))
-                for n, piece in enumerate(scores)
-            ]
+            terms = [jnp.exp2(score - top) for score in scores]
             plain = terms[0]
             for term in terms[1:]:
                 plain = plain + term
@@ -347,8 +344,7 @@
                 preferred_element_type=F32,
             )
             out = (mixed / norm).astype(BF16)
-            att[place, 0, :, cols] = out[:TOK_DEV]
-            att[place, 1, :, cols] = out[TOK_DEV:]
+            att[place : place + count, :, :, cols] = out.reshape(count, 2, TOK_DEV, HD)
 
     shared = {}
 
@@ -378,8 +374,7 @@
         return post(outbox.at[spot, piece], box.at[piece], at[to])
 
     own_clip(XFAR)
-    own_clip(XDOWN)
-    own_clip(XUP)
+    own_clip(XDOWN, 2)
     for copy in (right[1], left[0], over_right[1], over_left[0], *far):
         copy.wait_recv()
     earlier_clips(XFAR)
@@ -392,9 +387,8 @@
     fx0 = ship(XFAR, 0, fx, "up")
     fx1 = ship(XFAR, 1, fx, "down")
 
-    earlier_clips(XDOWN)
+    earlier_clips(XDOWN, 2)
     swap(XDOWN)
-    earlier_clips(XUP)
     swap(XUP)
     own_clip(FAR)
     multiply(XDOWN, XUP)
@@ -410,26 +404,23 @@
     fo0 = ship(FAR, 0, fo, "up")
     fo1 = ship(FAR, 1, fo, "down")
 
-    def rest(index, carry):
-        own_clip(index)
-        earlier_clips(index)
-        return carry
-
-    lax.fori_loop(DOWN, UP + 1, rest, 0)
+    own_clip(ACROSS)
+    earlier_clips(ACROSS)
+    swap(ACROSS)
+
+    own_clip(DOWN, 2)
+    earlier_clips(DOWN, 2)
     swap(DOWN)
     swap(UP)
-    own_clip(ACROSS)
-    multiply(DOWN, UP)
-    zd1 = ship(UP, 1, zd, "up")
-    zu0 = ship(DOWN, 0, zu, "down")
-    earlier_clips(ACROSS)
-    swap(ACROSS)
-    own_clip(OWN)
     multiply(ACROSS)
     cx1.wait_recv()
     ya1 = ship(ACROSS, 1, ya, "across", cx)
     cx0.wait_recv()
     ya0 = ship(ACROSS, 0, ya, "across", cx)
+    multiply(DOWN, UP)
+    zd1 = ship(UP, 1, zd, "up")
+    zu0 = ship(DOWN, 0, zu, "down")
+    own_clip(OWN)
     fo0.wait_recv()
     yx0.wait_recv()
     zd0 = ship(UP, 0, zd, "up", fo, yx)

time: 93.4 us -> 91 us (0.974)
  Pallas kernels: 92 us -> 89 us
    pallas_call x1, Pallas kernels: 90 us -> 87.1 us  [layer(): pl.pallas_call(layer_kernel, out_shape=(jax.ShapeDtypeStruct(lat.shape, B...]
where the time goes in v4:
time: 91 us; the launch traced here: 90.3 us
  Pallas kernels  89 us (98%)
  between operations  1.29 us (1%)
    pallas_call x1, Pallas kernels, layer(): pl.pallas_call(layer_kernel, out_shape=(jax.ShapeDtypeStruct(lat.shape, B...  87.1 us
    pallas_call x1, Pallas kernels, decode(): pl.pallas_call(decode_kernel, out_shape=(jax.ShapeDtypeStruct(den.shape,...  1.95 us

profile of v4, /device:TPU:0, one launch (start us, length us, event | category | flops | bytes accessed | tf_op | source)
XLA Modules:
  0.0 90.3 jit_solution(6518067058654131044)
XLA Ops:
  1.3 87.1 %layer.1 = (bf16[64,3584]{1,0:T(8,128)(2,1)}, bf16[80,128]{1,0:T(8,128)(2,1)}) custom-call(s32[1]{0:T(128)S(6)} %copy.12.levels, s32[8,8]{1,0:T(8,128)} %visible.1, s32[8]{0:T(128)} %counts.1, bf16[64,3584]{1,0:T(8,128)(2,1)} %bitcast.9, f32[3,16,3584]{2,1,0:T(8,128)} %bitcast.7, bf16[3,3584,256]{2,1,0:T(8,128)(2,1)} %bitcast.6, f32[2,256]{1,0:T(2,128)} %gain_in.1, ...), custom_call_target="tpu_custom_call" | custom-call | tf_op jit(solution)/shard_map/layer/pallas_call | solution.py:492
  88.4 1.9 %decode.1 = (bf16[64,3584]{1,0:T(8,128)(2,1)}, bf16[64,384]{1,0:T(8,128)(2,1)}) custom-call(bf16[64,3584]{1,0:T(8,128)(2,1)} %get-tuple-element.6.den_in, bf16[80,128]{1,0:T(8,128)(2,1)} %get-tuple-element.7.seq, bf16[3,96,384]{2,1,0:T(8,128)(2,1)} %conv_w.1), custom_call_target="tpu_custom_call" | custom-call | tf_op jit(solution)/shard_map/decode/pallas_call | solution.py:471
